TPU v7x, 512 devices: a whole 4x8x8 slice. The times are simulated.
512 devices in a mesh: leaf: 64 (over y, x, core), panel: 8 (over z).
Axes of the slice: x: 4, y: 8, z: 8, core: 2. Of those that a mesh axis runs over, the one named last changes fastest.
Arguments:
- rhs_0: bfloat16 [4096, 1024], P('leaf', 'panel'), may hold values from -6 to 6
- rhs_1: bfloat16 [4096, 1024], P('leaf', 'panel'), may hold values from -6 to 6
- rhs_2: bfloat16 [4096, 1024], P('leaf', 'panel'), may hold values from -6 to 6
- rhs_3: bfloat16 [4096, 1024], P('leaf', 'panel'), may hold values from -6 to 6
- inv_0: bfloat16 [4096, 4096], P(('leaf', 'panel')), as said below
- inv_1: bfloat16 [4096, 2048], P(('leaf', 'panel')), as said below
- inv_2: bfloat16 [4096, 1024], P(('leaf', 'panel')), as said below
- inv_3: bfloat16 [4096, 512], P(('leaf', 'panel')), as said below
- coupling_1: bfloat16 [4096, 2048], P(('leaf', 'panel')), may hold values from -0.125 to 0.125
- coupling_2: bfloat16 [4096, 1024], P(('leaf', 'panel')), may hold values from -0.1875 to 0.1875
- coupling_3: bfloat16 [4096, 512], P(('leaf', 'panel')), may hold values from -0.25 to 0.25
- update_rows_1: int32 [2, 2048], replicated, may hold values from 0 to 4095, as said below
- update_rows_2: int32 [4, 1024], replicated, may hold values from 0 to 6143, as said below
- update_rows_3: int32 [8, 512], replicated, may hold values from 0 to 7167, as said below
Outputs:
- solution_0: bfloat16 [4096, 1024], P('leaf', 'panel')
- solution_1: bfloat16 [4096, 1024], P('leaf', 'panel')
- solution_2: bfloat16 [4096, 1024], P('leaf', 'panel')
- solution_3: bfloat16 [4096, 1024], P('leaf', 'panel')
Inputs may be any that keep to these rules, and one draw needn't show every extreme that they name: `update_rows_1`: row f lists the update rows of front f of depth 1: 2048 distinct indices into its ancestor rows, holding 0 and the last ancestor row. `update_rows_2`: row f lists the update rows of front f of depth 2: 1024 distinct indices into its ancestor rows, holding 0 and the last ancestor row. `update_rows_3`: row f lists the update rows of front f of depth 3: 512 distinct indices into its ancestor rows, holding 0 and the last ancestor row. `inv_0`: the block is lower triangular with its diagonal between 0.5 and 2. `inv_1`: each 2048-row block is lower triangular with its diagonal between 0.5 and 2. `inv_2`: each 1024-row block is lower triangular with its diagonal between 0.5 and 2. `inv_3`: each 512-row block is lower triangular with its diagonal between 0.5 and 2.
All inputs are finite; a program needn't handle non-finite values.
Results may differ from a plain program's by a relative error of at most 0.014.
Values may be sent and summed in bfloat16 or wider, within the bound.
No kernel may reach another device: no remote copies, remote signals or barrier semaphores. Data moves between devices by JAX's collectives and lax.ppermute only.
A program may use at most 64 MiB of HBM per device.

v0:
```python
import jax
import jax.numpy as jnp
from jax import lax
from jax.sharding import PartitionSpec as P

PIVOTS = 4096
LEVELS = 4


def swapped(value, axis, bit):
    mask = 2**bit
    pairs = [(source, source ^ mask) for source in range(lax.axis_size(axis))]
    return lax.ppermute(value, axis, pairs)


def collect_rows(own_block, groups, front_rows):
    gathered = lax.all_gather(own_block, "leaf", axis=0, tiled=True)
    row_start = lax.axis_index("leaf") // groups * front_rows
    return lax.dynamic_slice_in_dim(gathered, row_start, front_rows, 0)


def halve_sums(block, groups):
    my_index = lax.axis_index("leaf")
    for bit_pos in reversed(range(groups.bit_length() - 1)):
        half_rows = block.shape[0] // 2
        lower_half = block[:half_rows]
        upper_half = block[half_rows:]
        is_high = my_index >> bit_pos & 1 == 1
        keep_part = jnp.where(is_high, upper_half, lower_half)
        send_part = jnp.where(is_high, lower_half, upper_half)
        block = keep_part + swapped(send_part, "leaf", bit_pos)
    return block


def reduce_rows(block, groups):
    return halve_sums(block, groups)


def contract_rows(left, right):
    return lax.dot_general(
        left, right, (((0,), (0,)), ((), ())), preferred_element_type=jnp.float32
    )


def body(
    rhs_0,
    rhs_1,
    rhs_2,
    rhs_3,
    inv_0,
    inv_1,
    inv_2,
    inv_3,
    coupling_1,
    coupling_2,
    coupling_3,
    update_rows_1,
    update_rows_2,
    update_rows_3,
):
    rhs_all = [rhs_0, rhs_1, rhs_2, rhs_3]
    lists_all = [None, update_rows_1, update_rows_2, update_rows_3]
    columns = rhs_0.shape[1]
    leaf_count = lax.axis_size("leaf")
    front_sizes = [PIVOTS >> depth_now for depth_now in range(LEVELS)]
    offsets = [0]
    for depth_now in range(1, LEVELS):
        offsets.append(offsets[-1] + front_sizes[depth_now - 1])
    fetched = (
        lax.all_gather(inv_0, "panel", axis=0, tiled=True),
        lax.all_gather(inv_1, "panel", axis=0, tiled=True),
        lax.all_gather(inv_2, "panel", axis=0, tiled=True),
        lax.all_gather(inv_3, "panel", axis=0, tiled=True),
        lax.all_gather(coupling_1, "panel", axis=0, tiled=True),
        lax.all_gather(coupling_2, "panel", axis=0, tiled=True),
        lax.all_gather(coupling_3, "panel", axis=0, tiled=True),
    )
    inv_rows_all = [fetched[0], fetched[1], fetched[2], fetched[3]]
    coup_rows_all = [None, fetched[4], fetched[5], fetched[6]]
    accumulated = jnp.zeros((offsets[LEVELS - 1], columns), jnp.float32)
    forwards = [None] * LEVELS
    for depth_now in reversed(range(LEVELS)):
        groups = leaf_count >> depth_now
        front_rows = front_sizes[depth_now]
        front = lax.axis_index("leaf") // groups
        summed = rhs_all[depth_now].astype(jnp.float32)
        if depth_now < LEVELS - 1:
            summed = summed + reduce_rows(
                accumulated[offsets[depth_now] : offsets[depth_now] + front_rows], groups
            )
        combined = collect_rows(summed.astype(jnp.bfloat16), groups, front_rows)
        values = jnp.dot(
            inv_rows_all[depth_now], combined, preferred_element_type=jnp.float32
        ).astype(jnp.bfloat16)
        forwards[depth_now] = values
        if depth_now > 0:
            update = contract_rows(coup_rows_all[depth_now], values)
            row_list = lax.dynamic_index_in_dim(lists_all[depth_now], front, 0, keepdims=False)
            accumulated = accumulated.at[row_list].add(update)
    anc_values = jnp.zeros((offsets[LEVELS - 1], columns), jnp.bfloat16)
    outputs = []
    for depth_now in range(LEVELS):
        groups = leaf_count >> depth_now
        front_rows = front_sizes[depth_now]
        front = lax.axis_index("leaf") // groups
        if depth_now > 0:
            row_list = lax.dynamic_index_in_dim(lists_all[depth_now], front, 0, keepdims=False)
            picked = jnp.take(anc_values, row_list, axis=0)
            pulled = jnp.dot(coup_rows_all[depth_now], picked, preferred_element_type=jnp.float32)
            adjusted = (forwards[depth_now].astype(jnp.float32) - pulled).astype(jnp.bfloat16)
        else:
            adjusted = forwards[depth_now]
        partial_value = contract_rows(inv_rows_all[depth_now], adjusted)
        solved = reduce_rows(partial_value, groups).astype(jnp.bfloat16)
        outputs.append(solved)
        if depth_now < LEVELS - 1:
            whole_front = collect_rows(solved, groups, front_rows)
            anc_values = anc_values.at[offsets[depth_now] : offsets[depth_now] + front_rows].set(
                whole_front
            )
    return (outputs[0], outputs[1], outputs[2], outputs[3])


def solution(mesh):
    in_specs = (
        P("leaf", "panel"),
        P("leaf", "panel"),
        P("leaf", "panel"),
        P("leaf", "panel"),
        P(("leaf", "panel"), None),
        P(("leaf", "panel"), None),
        P(("leaf", "panel"), None),
        P(("leaf", "panel"), None),
        P(("leaf", "panel"), None),
        P(("leaf", "panel"), None),
        P(("leaf", "panel"), None),
        P(),
        P(),
        P(),
    )
    out_specs = (P("leaf", "panel"), P("leaf", "panel"), P("leaf", "panel"), P("leaf", "panel"))
    return jax.shard_map(body, mesh=mesh, in_specs=in_specs, out_specs=out_specs, check_vma=False)
```

profile of v0, /device:TPU:1, one launch (start us, length us, event | category | flops | bytes accessed | tf_op | source)
XLA Modules:
  0.0 1056.7 jit_solution(4610110368345489924)
XLA Ops:
  8.0 25.9 %all_gather.43 = bf16[64,512]{1,0:T(8,128)(2,1)S(1)} all-gather(bf16[8,512]{1,0:T(8,128)(2,1)} %param.27), channel_id=1, replica_groups=mesh['leaf'=64,'panel'=8] {'panel'}, dimensions={0}, use_global_device_ids=true | all-gather | bytes 73728 | tf_op jit(solution)/shard_map/all_gather | solution.py:73
  33.9 19.2 %all_gather.44 = bf16[64,512]{1,0:T(8,128)(2,1)S(1)} all-gather(bf16[8,512]{1,0:T(8,128)(2,1)} %param.30), channel_id=1, replica_groups=mesh['leaf'=64,'panel'=8] {'panel'}, dimensions={0}, use_global_device_ids=true | all-gather | bytes 73728 | tf_op jit(solution)/shard_map/all_gather | solution.py:76
  54.4 44.7 %all-gather.8.cloned.1.call-done = bf16[4096,128]{1,0:T(8,128)(2,1)} async-done(((bf16[64,128]{1,0:T(8,128)(2,1)}), bf16[4096,128]{1,0:T(8,128)(2,1)}) %all-gather.8.cloned.1.call-update) | async-done | bytes 1048592 | tf_op jit(solution)/shard_map/all_gather | solution.py:17
  108.7 7.2 collective-permute-done
  136.3 20.5 %all_gather.46 = bf16[64,1024]{1,0:T(8,128)(2,1)S(1)} all-gather(bf16[8,1024]{1,0:T(8,128)(2,1)S(1)} %copy-done.13), channel_id=1, replica_groups=mesh['leaf'=64,'panel'=8] {'panel'}, dimensions={0}, use_global_device_ids=true | all-gather | bytes 147456 | tf_op jit(solution)/shard_map/all_gather | solution.py:72
  156.8 19.3 %all_gather.47 = bf16[64,1024]{1,0:T(8,128)(2,1)S(1)} all-gather(bf16[8,1024]{1,0:T(8,128)(2,1)S(1)} %copy-done.14), channel_id=1, replica_groups=mesh['leaf'=64,'panel'=8] {'panel'}, dimensions={0}, use_global_device_ids=true | all-gather | bytes 147456 | tf_op jit(solution)/shard_map/all_gather | solution.py:75
  177.4 39.1 %all-gather.10.cloned.1.call-done = bf16[4096,128]{1,0:T(8,128)(2,1)} async-done(((bf16[64,128]{1,0:T(8,128)(2,1)}), bf16[4096,128]{1,0:T(8,128)(2,1)}) %all-gather.10.cloned.1.call-update) | async-done | bytes 1048592 | tf_op jit(solution)/shard_map/all_gather | solution.py:17
  218.1 9.3 scatter_fusion
  232.6 23.9 %collective-permute-done.4 = f32[1024,128]{1,0:T(8,128)S(1)} collective-permute-done((f32[1024,128]{1,0:T(8,128)S(1)}, f32[1024,128]{1,0:T(8,128)S(1)}, u32[]{:S(2)}, u32[]{:S(2)}) %collective-permute-start.4) | collective-permute-done | bytes 524320 | tf_op jit(solution)/shard_map/ppermute | solution.py:13
  259.8 7.3 collective-permute-done.5
  286.6 20.6 %all_gather.49 = bf16[64,2048]{1,0:T(8,128)(2,1)S(1)} all-gather(bf16[8,2048]{1,0:T(8,128)(2,1)S(1)} %copy-done.11), channel_id=1, replica_groups=mesh['leaf'=64,'panel'=8] {'panel'}, dimensions={0}, use_global_device_ids=true | all-gather | bytes 294912 | tf_op jit(solution)/shard_map/all_gather | solution.py:71
  307.3 20.0 %all_gather.50 = bf16[64,2048]{1,0:T(8,128)(2,1)S(1)} all-gather(bf16[8,2048]{1,0:T(8,128)(2,1)S(1)} %copy-done.12), channel_id=1, replica_groups=mesh['leaf'=64,'panel'=8] {'panel'}, dimensions={0}, use_global_device_ids=true | all-gather | bytes 294912 | tf_op jit(solution)/shard_map/all_gather | solution.py:74
  327.3 39.1 %all-gather.12.cloned.1.call-done = bf16[4096,128]{1,0:T(8,128)(2,1)} async-done(((bf16[64,128]{1,0:T(8,128)(2,1)}), bf16[4096,128]{1,0:T(8,128)(2,1)}) %all-gather.12.cloned.1.call-update) | async-done | bytes 1048592 | tf_op jit(solution)/shard_map/all_gather | solution.py:17
  368.3 14.2 %scatter_fusion.1 = f32[7168,128]{1,0:T(8,128)} fusion(f32[7168,128]{1,0:T(8,128)} %scatter_fusion, s32[2048]{0:T(1024)S(1)} %bitcast.44, f32[2048,128]{1,0:T(8,128)S(1)} %copy.80), kind=kCustom, calls=%fused_computation.5 | custom fusion | flops 262144 | bytes 3153920 | tf_op jit(solution)/shard_map/scatter-add | solution.py:99
  388.9 32.4 %collective-permute-done.9 = f32[2048,128]{1,0:T(8,128)S(1)} collective-permute-done((f32[2048,128]{1,0:T(8,128)S(1)}, f32[2048,128]{1,0:T(8,128)S(1)}, u32[]{:S(2)}, u32[]{:S(2)}) %collective-permute-start.9) | collective-permute-done | bytes 1048608 | tf_op jit(solution)/shard_map/ppermute | solution.py:13
  423.1 19.9 %collective-permute-start.10 = (f32[1024,128]{1,0:T(8,128)S(1)}, f32[1024,128]{1,0:T(8,128)S(1)}, u32[]{:S(2)}, u32[]{:S(2)}) collective-permute-start(f32[1024,128]{1,0:T(8,128)S(1)} %slice_select_fusion.4), channel_id=1, source_target_pairs={{0,128},{8,136},{16,144},{24,152},{32,160},{40,168},{48,176},{56,1... | collective-permute-start | bytes 1572872 | tf_op jit(solution)/shard_map/ppermute | solution.py:13
  443.1 23.3 %collective-permute-done.10 = f32[1024,128]{1,0:T(8,128)S(1)} collective-permute-done((f32[1024,128]{1,0:T(8,128)S(1)}, f32[1024,128]{1,0:T(8,128)S(1)}, u32[]{:S(2)}, u32[]{:S(2)}) %collective-permute-start.10) | collective-permute-done | bytes 524320 | tf_op jit(solution)/shard_map/ppermute | solution.py:13
  468.4 7.4 collective-permute-done.11
  495.3 22.4 %all_gather.52 = bf16[64,4096]{1,0:T(8,128)(2,1)S(1)} all-gather(bf16[8,4096]{1,0:T(8,128)(2,1)S(1)} %copy-done.9), channel_id=1, replica_groups=mesh['leaf'=64,'panel'=8] {'panel'}, dimensions={0}, use_global_device_ids=true | all-gather | bytes 589824 | tf_op jit(solution)/shard_map/all_gather | solution.py:70
  517.7 57.2 %all-gather.14.cloned.1.call-done = bf16[4096,128]{1,0:T(8,128)(2,1)} async-done(((bf16[64,128]{1,0:T(8,128)(2,1)}), bf16[4096,128]{1,0:T(8,128)(2,1)}) %all-gather.14.cloned.1.call-update) | async-done | bytes 1048592 | tf_op jit(solution)/shard_map/all_gather | solution.py:17
  581.9 32.4 %collective-permute-done.15 = f32[2048,128]{1,0:T(8,128)S(1)} collective-permute-done((f32[2048,128]{1,0:T(8,128)S(1)}, f32[2048,128]{1,0:T(8,128)S(1)}, u32[]{:S(2)}, u32[]{:S(2)}) %collective-permute-start.15) | collective-permute-done | bytes 1048608 | tf_op jit(solution)/shard_map/ppermute | solution.py:13
  614.5 19.9 %collective-permute-start.16 = (f32[1024,128]{1,0:T(8,128)S(1)}, f32[1024,128]{1,0:T(8,128)S(1)}, u32[]{:S(2)}, u32[]{:S(2)}) collective-permute-start(f32[1024,128]{1,0:T(8,128)S(1)} %slice_select_fusion.3), channel_id=1, source_target_pairs={{0,128},{8,136},{16,144},{24,152},{32,160},{40,168},{48,176},{56,1... | collective-permute-start | bytes 1572872 | tf_op jit(solution)/shard_map/ppermute | solution.py:13
  634.4 23.3 %collective-permute-done.16 = f32[1024,128]{1,0:T(8,128)S(1)} collective-permute-done((f32[1024,128]{1,0:T(8,128)S(1)}, f32[1024,128]{1,0:T(8,128)S(1)}, u32[]{:S(2)}, u32[]{:S(2)}) %collective-permute-start.16) | collective-permute-done | bytes 524320 | tf_op jit(solution)/shard_map/ppermute | solution.py:13
  659.8 7.4 collective-permute-done.17
  687.2 79.0 %all-gather.16.cloned.1.call-done = bf16[4096,128]{1,0:T(8,128)(2,1)} async-done(((bf16[64,128]{1,0:T(8,128)(2,1)}), bf16[4096,128]{1,0:T(8,128)(2,1)}) %all-gather.16.cloned.1.call-update) | async-done | bytes 1048592 | tf_op jit(solution)/shard_map/all_gather | solution.py:17
  767.7 8.0 gather_fusion
  781.5 23.9 %collective-permute-done.21 = f32[1024,128]{1,0:T(8,128)S(1)} collective-permute-done((f32[1024,128]{1,0:T(8,128)S(1)}, f32[1024,128]{1,0:T(8,128)S(1)}, u32[]{:S(2)}, u32[]{:S(2)}) %collective-permute-start.21) | collective-permute-done | bytes 524320 | tf_op jit(solution)/shard_map/ppermute | solution.py:13
  807.6 7.3 collective-permute-done.22
  827.3 5.6 collective-permute-start.25
  835.8 78.3 %all-gather.18.cloned.1.call-done = bf16[4096,128]{1,0:T(8,128)(2,1)} async-done(((bf16[64,128]{1,0:T(8,128)(2,1)}), bf16[4096,128]{1,0:T(8,128)(2,1)}) %all-gather.18.cloned.1.call-update) | async-done | bytes 1048592 | tf_op jit(solution)/shard_map/all_gather | solution.py:17
  921.4 7.2 collective-permute-done.26
  947.8 80.3 %all-gather.20.cloned.1.call-done = bf16[4096,128]{1,0:T(8,128)(2,1)} async-done(((bf16[64,128]{1,0:T(8,128)(2,1)}), bf16[4096,128]{1,0:T(8,128)(2,1)}) %all-gather.20.cloned.1.call-update) | async-done | bytes 1048592 | tf_op jit(solution)/shard_map/all_gather | solution.py:17
  (203 shorter events, 195.8 us)
Async XLA Ops:
  7.2 92.0 %all-gather.8.cloned.1.call-start = ((), (), s32[]{:S(2)}) async-start(), calls=%async_computation | async-start | bytes 1064960 | tf_op jit(solution)/shard_map/all_gather | solution.py:17
  7.9 208.6 %all-gather.10.cloned.1.call-start = ((), (), s32[]{:S(2)}) async-start(), calls=%async_computation.1 | async-start | bytes 1064960 | tf_op jit(solution)/shard_map/all_gather | solution.py:17
  106.5 9.5 collective-permute-start
  117.1 7.2 collective-permute-start.1
  129.4 6.2 collective-permute-start.3
  136.2 230.1 %all-gather.12.cloned.1.call-start = ((), (), s32[]{:S(2)}) async-start(), calls=%async_computation.2 | async-start | bytes 1064960 | tf_op jit(solution)/shard_map/all_gather | solution.py:17
  228.7 27.8 %collective-permute-start.4 = (f32[1024,128]{1,0:T(8,128)S(1)}, f32[1024,128]{1,0:T(8,128)S(1)}, u32[]{:S(2)}, u32[]{:S(2)}) collective-permute-start(f32[1024,128]{1,0:T(8,128)S(1)} %slice_select_fusion.5), channel_id=1, source_target_pairs={{0,128},{8,136},{16,144},{24,152},{32,160},{40,168},{48,176},{56,1... | collective-permute-start | bytes 1572872 | tf_op jit(solution)/shard_map/ppermute | solution.py:13
  257.9 9.2 collective-permute-start.5
  267.2 7.2 collective-permute-start.6
  279.5 6.4 collective-permute-start.8
  286.6 288.4 %all-gather.14.cloned.1.call-start = ((), (), s32[]{:S(2)}) async-start(), calls=%async_computation.3 | async-start | bytes 1064960 | tf_op jit(solution)/shard_map/all_gather | solution.py:17
  384.1 37.3 %collective-permute-start.9 = (f32[2048,128]{1,0:T(8,128)S(1)}, f32[2048,128]{1,0:T(8,128)S(1)}, u32[]{:S(2)}, u32[]{:S(2)}) collective-permute-start(f32[2048,128]{1,0:T(8,128)S(1)} %slice_select_fusion.1), channel_id=1, source_target_pairs={{0,256},{8,264},{16,272},{24,280},{32,288},{40,296},{48,304},{56,3... | collective-permute-start | bytes 3145736 | tf_op jit(solution)/shard_map/ppermute | solution.py:13
  423.1 43.3 %collective-permute-start.10 = (f32[1024,128]{1,0:T(8,128)S(1)}, f32[1024,128]{1,0:T(8,128)S(1)}, u32[]{:S(2)}, u32[]{:S(2)}) collective-permute-start(f32[1024,128]{1,0:T(8,128)S(1)} %slice_select_fusion.4), channel_id=1, source_target_pairs={{0,128},{8,136},{16,144},{24,152},{32,160},{40,168},{48,176},{56,1... | collective-permute-start | bytes 1572872 | tf_op jit(solution)/shard_map/ppermute | solution.py:13
  466.5 9.3 collective-permute-start.11
  475.9 7.2 collective-permute-start.12
  488.2 6.4 collective-permute-start.14
  495.2 271.0 %all-gather.16.cloned.1.call-start = ((), (), s32[]{:S(2)}) async-start(), calls=%async_computation.4 | async-start | bytes 1064960 | tf_op jit(solution)/shard_map/all_gather | solution.py:17
  577.0 37.3 %collective-permute-start.15 = (f32[2048,128]{1,0:T(8,128)S(1)}, f32[2048,128]{1,0:T(8,128)S(1)}, u32[]{:S(2)}, u32[]{:S(2)}) collective-permute-start(f32[2048,128]{1,0:T(8,128)S(1)} %slice_select_fusion), channel_id=1, source_target_pairs={{0,256},{8,264},{16,272},{24,280},{32,288},{40,296},{48,304},{56,3... | collective-permute-start | bytes 3145736 | tf_op jit(solution)/shard_map/ppermute | solution.py:13
  614.5 43.3 %collective-permute-start.16 = (f32[1024,128]{1,0:T(8,128)S(1)}, f32[1024,128]{1,0:T(8,128)S(1)}, u32[]{:S(2)}, u32[]{:S(2)}) collective-permute-start(f32[1024,128]{1,0:T(8,128)S(1)} %slice_select_fusion.3), channel_id=1, source_target_pairs={{0,128},{8,136},{16,144},{24,152},{32,160},{40,168},{48,176},{56,1... | collective-permute-start | bytes 1572872 | tf_op jit(solution)/shard_map/ppermute | solution.py:13
  657.9 9.3 collective-permute-start.17
  667.3 7.2 collective-permute-start.18
  679.6 6.4 collective-permute-start.20
  686.6 227.5 %all-gather.18.cloned.1.call-start = ((), (), s32[]{:S(2)}) async-start(), calls=%async_computation.5 | async-start | bytes 1064960 | tf_op jit(solution)/shard_map/all_gather | solution.py:17
  777.6 27.8 %collective-permute-start.21 = (f32[1024,128]{1,0:T(8,128)S(1)}, f32[1024,128]{1,0:T(8,128)S(1)}, u32[]{:S(2)}, u32[]{:S(2)}) collective-permute-start(f32[1024,128]{1,0:T(8,128)S(1)} %slice_select_fusion.2), channel_id=1, source_target_pairs={{0,128},{8,136},{16,144},{24,152},{32,160},{40,168},{48,176},{56,1... | collective-permute-start | bytes 1572872 | tf_op jit(solution)/shard_map/ppermute | solution.py:13
  805.5 9.4 collective-permute-start.22
  815.0 7.2 collective-permute-start.23
  827.3 6.4 collective-permute-start.25
  834.4 193.8 %all-gather.20.cloned.1.call-start = ((), (), s32[]{:S(2)}) async-start(), calls=%async_computation.6 | async-start | bytes 1064960 | tf_op jit(solution)/shard_map/all_gather | solution.py:17
  919.1 9.5 collective-permute-start.26
  928.7 7.2 collective-permute-start.27
  941.0 6.2 collective-permute-start.29
  1030.9 8.2 collective-permute-start.30
  (30 other events, 1452.1 us)
Sparse Core Ops, SparseCore 0:
  11.3 87.8 all-gather.7
  136.4 80.1 all-gather.9
  286.7 79.5 all-gather.11
  495.3 79.5 all-gather.13
  686.7 79.4 all-gather.15
  834.5 79.6 all-gather.17
  947.9 80.1 all-gather.19
where the time goes:
time: 1060 us
  waiting for transfers between devices  676 us (64%)
  blocking collectives  148 us (14%)
  starting transfers between devices  145 us (14%)
  other arithmetic  46.2 us (4%)
  local copies, waits for them, and re-layouts  17.4 us (2%)
  between operations  15.2 us (1%)
    all_gather x7, waiting for transfers between devices, collect_rows(): gathered = lax.all_gather(own_block, 'leaf', axis=0, tiled=True)  418 us
    ppermute x33, waiting for transfers between devices, swapped(): return lax.ppermute(value, axis, pairs)  257 us
    ppermute x33, starting transfers between devices, swapped(): return lax.ppermute(value, axis, pairs)  145 us
    scatter-add x3, other arithmetic, body(): accumulated = accumulated.at[row_list].add(update)  27.6 us
    all_gather x1, blocking collectives, body(): lax.all_gather(inv_3, 'panel', axis=0, tiled=True)  25.9 us
    all_gather x1, blocking collectives, body(): lax.all_gather(inv_0, 'panel', axis=0, tiled=True)  22.4 us
  transfers between devices with their start and end apart: 40, of which 40 were waited for; matrix products, arithmetic and copies ran while one was open for 0% of the time, Pallas kernels for 0%

commit v1 on v0

v1 whole, which is shorter than its diff:
```python
import functools

import jax
import jax.numpy as jnp
from jax import lax
from jax.experimental import pallas as pl
from jax.sharding import Mesh
from jax.sharding import PartitionSpec as P

PIVOTS = 4096
LEVELS = 4
BLOCK = 128
HALF = 64
CHUNK = 256
INTERPRET = False

CHIPS = ("ya", "yb", "yc", "x")
GROUP_AXES = (CHIPS, CHIPS[1:], CHIPS[2:], CHIPS[3:])
GROUP_SIZE = (32, 16, 8, 4)
LEAF = ("ya", "yb", "yc", "x", "c")


def exchange(value, axes):
    return lax.all_to_all(value, axes, 0, 0, tiled=True)


def dot_nt(left, right):
    return lax.dot_general(left, right, (((1,), (1,)), ((), ())), preferred_element_type=jnp.float32)


def dot_nn(left, right):
    return lax.dot_general(left, right, (((1,), (0,)), ((), ())), preferred_element_type=jnp.float32)


def call(kernel, out_shapes, inputs):
    specs = []
    arrays = []
    for item in inputs:
        array, shape, index = item if isinstance(item, tuple) else (item, item.shape, (0,) * item.ndim)
        specs.append(pl.BlockSpec(shape, functools.partial(lambda at, _: at, index)))
        arrays.append(array)
    out_specs = [pl.BlockSpec(o.shape, functools.partial(lambda at, _: at, (0,) * len(o.shape))) for o in out_shapes]
    return pl.pallas_call(
        kernel, grid=(1,), in_specs=specs, out_specs=out_specs, out_shape=out_shapes, interpret=INTERPRET
    )(*arrays)


def bf16(*shape):
    return jax.ShapeDtypeStruct(shape, jnp.bfloat16)


def expand_kernel(list_ref, block_ref, out_ref):
    block = block_ref[...]
    rows = list_ref[...]
    width = block.shape[1]
    lane = lax.broadcasted_iota(jnp.int32, (CHUNK, width), 0).astype(jnp.float32).astype(jnp.bfloat16)

    def step(at, carry):
        shifted = jnp.clip(rows - at * CHUNK, -1, CHUNK).astype(jnp.float32).astype(jnp.bfloat16)
        hit = jnp.where(shifted == lane, jnp.bfloat16(1), jnp.bfloat16(0))
        out_ref[pl.ds(pl.multiple_of(at * CHUNK, CHUNK), CHUNK), :] = dot_nt(hit, block).astype(jnp.bfloat16)
        return carry

    lax.fori_loop(0, out_ref.shape[0] // CHUNK, step, 0)


def expanded(row_list, block_item, ancestors):
    return call(expand_kernel, [bf16(ancestors, BLOCK)], [row_list, block_item])[0]


def pairs_product(full_ref, weights, count):
    total = None
    for at in range(0, count, 2):
        left = jnp.concatenate([full_ref[at], full_ref[at + 1]], axis=1)
        part = weights(left, at)
        total = part if total is None else total + part
    return total


def front_values(full_ref, inv_ref, count):
    return pairs_product(
        full_ref, lambda left, at: dot_nt(left, inv_ref[:, at * BLOCK : (at + 2) * BLOCK]), count
    ).astype(jnp.bfloat16)


def forward_kernel(deeper, count, send_count, *refs):
    full_ref, inv_ref = refs[:2]
    old = refs[2 : 2 + deeper]
    couplings = refs[2 + deeper : 3 + 2 * deeper]
    values_ref, send_ref = refs[-2:]
    values = front_values(full_ref, inv_ref, count)
    values_ref[...] = values
    stacked = [r[...] for r in old] + [values]
    for at in range(send_count):
        total = None
        for left, ref in zip(stacked, couplings):
            part = dot_nt(left, ref[at * BLOCK : (at + 1) * BLOCK, :])
            total = part if total is None else total + part
        send_ref[at] = total.astype(jnp.bfloat16)


def spread_kernel(count, has_own, *refs):
    parts_ref = refs[0]
    total = refs[1][...].astype(jnp.float32) if has_own else None
    for at in range(count):
        part = parts_ref[at].astype(jnp.float32)
        total = part if total is None else total + part
    result = total.astype(jnp.bfloat16)
    out_ref = refs[1 + has_own]
    if len(refs) > 2 + has_own:
        refs[-1][...] = result
    if len(out_ref.shape) == 2:
        out_ref[...] = result
    else:
        for at in range(count):
            out_ref[at] = result


def root_kernel(full_ref, inv_ref, send_ref):
    values = front_values(full_ref, inv_ref, GROUP_SIZE[0])
    for at in range(GROUP_SIZE[0]):
        send_ref[at] = dot_nn(values, inv_ref[:, at * BLOCK : (at + 1) * BLOCK]).astype(jnp.bfloat16)


def backward_kernel(depth, *refs):
    solved = refs[:depth]
    values_ref, coupling_ref, inv_ref, send_ref = refs[depth:]
    total = values_ref[...].astype(jnp.float32)
    start = 0
    for upper in range(depth):
        base = start

        def product(left, at):
            return dot_nn(left, coupling_ref[base + at * BLOCK : base + (at + 2) * BLOCK, :])

        total = total - pairs_product(solved[upper], product, GROUP_SIZE[upper])
        start += GROUP_SIZE[upper] * BLOCK
    adjusted = total.astype(jnp.bfloat16)
    for at in range(GROUP_SIZE[depth]):
        send_ref[at] = dot_nn(adjusted, inv_ref[:, at * BLOCK : (at + 1) * BLOCK]).astype(jnp.bfloat16)


def gather_rows(parts):
    shard = jnp.concatenate(parts, axis=1)
    panels = lax.axis_size("z")
    rows = exchange(jnp.broadcast_to(shard[None], (panels,) + shard.shape), "z")
    rows = rows.reshape(panels * shard.shape[0], shard.shape[1])
    both = exchange(jnp.broadcast_to(rows[None], (2,) + rows.shape), "c")
    return both.reshape(BLOCK, shard.shape[1])


def body(
    rhs_0, rhs_1, rhs_2, rhs_3, inv_0, inv_1, inv_2, inv_3, coupling_1, coupling_2, coupling_3, rows_1, rows_2, rows_3
):
    stacked = jnp.concatenate([rhs_0, rhs_1, rhs_2, rhs_3], axis=0).T
    halves = exchange(stacked.reshape(2, HALF, 4 * HALF), "c")
    rhs = [
        jnp.concatenate([halves[0][:, k * HALF : (k + 1) * HALF], halves[1][:, k * HALF : (k + 1) * HALF]], axis=1)
        for k in range(LEVELS)
    ]
    low = gather_rows([inv_1, coupling_1, inv_2, coupling_2, inv_3, coupling_3])
    top = gather_rows([inv_0])
    inv = [
        (top, (BLOCK, 4096), (0, 0)),
        (low, (BLOCK, 2048), (0, 0)),
        (low, (BLOCK, 1024), (0, 4)),
        (low, (BLOCK, 512), (0, 12)),
    ]
    coup = [None, (low, (BLOCK, 2048), (0, 1)), (low, (BLOCK, 1024), (0, 5)), (low, (BLOCK, 512), (0, 13))]
    chip = lax.axis_index(CHIPS)
    exp = [None]
    ancestors = 0
    for k, lists in ((1, rows_1), (2, rows_2), (3, rows_3)):
        ancestors += PIVOTS >> (k - 1)
        mine = lax.dynamic_slice_in_dim(lists, chip // GROUP_SIZE[k], 1, 0)
        exp.append(expanded(mine, coup[k], ancestors))

    def spread(parts, own, count, keep):
        outs = [bf16(count, HALF, BLOCK)] + ([bf16(HALF, BLOCK)] if keep else [])
        kernel = functools.partial(spread_kernel, count, int(own is not None))
        return call(kernel, outs, [parts] + ([own] if own is not None else []))

    values = [None] * LEVELS
    sent = jnp.broadcast_to(rhs[3][None], (4, HALF, BLOCK))
    for k in (3, 2, 1):
        full = exchange(sent, GROUP_AXES[k])
        send_count = GROUP_SIZE[k - 1]
        where = sum(PIVOTS >> j for j in range(k - 1)) // (PIVOTS >> (k - 1))
        order = list(range(3, k, -1))
        blocks = [(exp[j], (PIVOTS >> (k - 1), BLOCK), (where, 0)) for j in order + [k]]
        values[k], parts = call(
            functools.partial(forward_kernel, len(order), GROUP_SIZE[k], send_count),
            [bf16(HALF, BLOCK), bf16(send_count, HALF, BLOCK)],
            [full, inv[k]] + [values[j] for j in order] + blocks,
        )
        parts = exchange(parts, GROUP_AXES[k - 1])
        (sent,) = spread(parts, rhs[k - 1], send_count, False)
    full = exchange(sent, CHIPS)
    parts = call(root_kernel, [bf16(GROUP_SIZE[0], HALF, BLOCK)], [full, inv[0]])[0]
    solved = []
    out = []
    for k in range(LEVELS):
        parts = exchange(parts, GROUP_AXES[k])
        if k == LEVELS - 1:
            kernel = functools.partial(spread_kernel, GROUP_SIZE[k], 0)
            out.append(call(kernel, [bf16(HALF, BLOCK)], [parts])[0])
            break
        sent, own = spread(parts, None, GROUP_SIZE[k], True)
        out.append(own)
        solved.append(exchange(sent, GROUP_AXES[k]))
        parts = call(
            functools.partial(backward_kernel, k + 1),
            [bf16(GROUP_SIZE[k + 1], HALF, BLOCK)],
            solved + [values[k + 1], exp[k + 1], inv[k + 1]],
        )[0]
    halves = jnp.stack(
        [jnp.concatenate([o[:, h * HALF : (h + 1) * HALF] for o in out], axis=1) for h in range(2)], axis=0
    )
    rows = exchange(halves, "c").reshape(2 * HALF, 4 * HALF).T
    return tuple(rows[k * HALF : (k + 1) * HALF] for k in range(LEVELS))


def solution(mesh):
    devices = mesh.devices
    fine = Mesh(devices.reshape(2, 2, 2, 4, 2, devices.size // 64), ("ya", "yb", "yc", "x", "c", "z"))
    wide = P(LEAF, "z")
    rows = P(LEAF + ("z",), None)
    return jax.shard_map(
        body,
        mesh=fine,
        in_specs=(wide,) * 4 + (rows,) * 7 + (P(None, None),) * 3,
        out_specs=(wide,) * 4,
        check_vma=False,
    )
```

time: 1060 us -> 338 us (0.32)
  waiting for transfers between devices: 676 us -> 60.9 us
  starting transfers between devices: 145 us -> 59.4 us
  Pallas kernels: 0 us -> 62.4 us
  other arithmetic: 46.2 us -> 3.11 us
  blocking collectives: 148 us -> 131 us
  between operations: 15.2 us -> 0.83 us
    all_gather x7 -> x0, waiting for transfers between devices: 418 us -> none  [collect_rows(): gathered = lax.all_gather(own_block, 'leaf', axis=0, tiled=True)]
    ppermute x33 -> x0, waiting for transfers between devices: 257 us -> none  [swapped(): return lax.ppermute(value, axis, pairs)]
    all_gather x7 -> x0, blocking collectives: 148 us -> none  [the longest x1 25.9 us: body(): lax.all_gather(inv_3, 'panel', axis=0, tiled=True)]
    ppermute x33 -> x0, starting transfers between devices: 145 us -> none  [swapped(): return lax.ppermute(value, axis, pairs)]
    all_to_all x0 -> x9, blocking collectives: none -> 131 us  [exchange(): return lax.all_to_all(value, axes, 0, 0, tiled=True)]
    pallas_call x0 -> x17, Pallas kernels: none -> 62.4 us  [call(): pl.pallas_call(kernel, grid=(1,), in_specs=specs, out_specs=out_specs, ou...]
    all_to_all x0 -> x11, waiting for transfers between devices: none -> 60.9 us  [exchange(): return lax.all_to_all(value, axes, 0, 0, tiled=True)]
    all_to_all x0 -> x11, starting transfers between devices: none -> 59.4 us  [exchange(): return lax.all_to_all(value, axes, 0, 0, tiled=True)]
  transfers between devices with their start and end apart: 40 -> 11, of which waited for: 40 -> 6; matrix products, arithmetic and copies ran while one was open for 0% -> 3% of each run, Pallas kernels for 0% -> 10%
where the time goes in v1:
time: 338 us; the launch traced here: 335 us
  blocking collectives  131 us (39%)
  Pallas kernels  62.4 us (18%)
  waiting for transfers between devices  60.9 us (18%)
  starting transfers between devices  59.4 us (18%)
  local copies, waits for them, and re-layouts  17.9 us (5%)
    all_to_all x9, blocking collectives, exchange(): return lax.all_to_all(value, axes, 0, 0, tiled=True)  131 us
    pallas_call x17, Pallas kernels, call(): pl.pallas_call(kernel, grid=(1,), in_specs=specs, out_specs=out_specs, ou...  62.4 us
    all_to_all x11, waiting for transfers between devices, exchange(): return lax.all_to_all(value, axes, 0, 0, tiled=True)  60.9 us
    all_to_all x11, starting transfers between devices, exchange(): return lax.all_to_all(value, axes, 0, 0, tiled=True)  59.4 us
    unnamed x31, local copies, waits for them, and re-layouts  7.56 us
  transfers between devices with their start and end apart: 11, of which 6 were waited for; matrix products, arithmetic and copies ran while one was open for 3% of the time, Pallas kernels for 10%

profile of v1, /device:TPU:1, one launch (start us, length us, event | category | flops | bytes accessed | tf_op | source)
XLA Modules:
  0.0 335.5 jit_solution(10080704297919864618)
XLA Ops:
  2.2 10.1 %all-to-all-start = ((bf16[2,64,256]{2,1,0:T(8,128)(2,1)}), bf16[2,64,256]{2,1,0:T(8,128)(2,1)S(1)}, u32[]{:S(2)}, u32[]{:S(2)}) async-start(bf16[2,64,256]{2,1,0:T(8,128)(2,1)} %bitcast.1), calls=%async_computation | async-start | bytes 131072 | tf_op jit(solution)/shard_map/all_to_all | solution.py:24
  17.6 4.7 %all-to-all-start.2 = ((bf16[8,8,7168]{2,1,0:T(8,128)(2,1)}), bf16[8,8,7168]{2,1,0:T(8,128)(2,1)S(1)}, u32[]{:S(2)}, u32[]{:S(2)}) async-start(bf16[8,8,7168]{2,1,0:T(8,128)(2,1)} %broadcast_in_dim.15), calls=%async_computation.2 | async-start | bytes 1835008 | tf_op jit(solution)/shard_map/all_to_all | solution.py:24
  22.5 26.2 %all-to-all-done.2 = bf16[8,8,7168]{2,1,0:T(8,128)(2,1)S(1)} async-done(((bf16[8,8,7168]{2,1,0:T(8,128)(2,1)}), bf16[8,8,7168]{2,1,0:T(8,128)(2,1)S(1)}, u32[]{:S(2)}, u32[]{:S(2)}) %all-to-all-start.2) | async-done | bytes 917536 | tf_op jit(solution)/shard_map/all_to_all | solution.py:24
  48.9 6.2 %all_to_all.100 = bf16[2,64,7168]{2,1,0:T(8,128)(2,1)} all-to-all(bf16[2,64,7168]{2,1,0:T(8,128)(2,1)S(1)} %broadcast_in_dim.17), channel_id=1, replica_groups=mesh['ya'=2,'yb'=2,'yc'=2,'x'=4,'c'=2,'z'=8] {'c'}, dimensions={0} | all-to-all | bytes 3670016 | tf_op jit(solution)/shard_map/all_to_all | solution.py:24
  55.7 4.0 %all-to-all-start.1 = ((bf16[4,64,128]{2,1,0:T(8,128)(2,1)}), bf16[4,64,128]{2,1,0:T(8,128)(2,1)S(1)}, u32[]{:S(2)}, u32[]{:S(2)}) async-start(bf16[4,64,128]{2,1,0:T(8,128)(2,1)} %broadcast_in_dim.14), calls=%async_computation.1 | async-start | bytes 131072 | tf_op jit(solution)/shard_map/all_to_all | solution.py:24
  61.0 8.8 %shard_map.165.refs_2_.refs_3_.refs_4_ = bf16[7168,128]{1,0:T(8,128)(2,1)} custom-call(s32[1,512]{1,0:T(1,128)} %constant_dynamic-slice_fusion.2.list_ref, bf16[128,7168]{1,0:T(8,128)(2,1)} %bitcast.17), custom_call_target="tpu_custom_call" | custom-call | tf_op jit(solution)/shard_map/pallas_call | solution.py:43
  72.6 5.3 %all-to-all-start.4 = ((bf16[8,64,128]{2,1,0:T(8,128)(2,1)}), bf16[8,64,128]{2,1,0:T(8,128)(2,1)S(1)}, u32[]{:S(2)}, u32[]{:S(2)}) async-start(bf16[8,64,128]{2,1,0:T(8,128)(2,1)} %get-tuple-element.16), calls=%async_computation.4 | async-start | bytes 262144 | tf_op jit(solution)/shard_map/all_to_all | solution.py:24
  78.5 4.7 %all-to-all-done.4.refs_0_ = bf16[8,64,128]{2,1,0:T(8,128)(2,1)S(1)} async-done(((bf16[8,64,128]{2,1,0:T(8,128)(2,1)}), bf16[8,64,128]{2,1,0:T(8,128)(2,1)S(1)}, u32[]{:S(2)}, u32[]{:S(2)}) %all-to-all-start.4) | async-done | bytes 131104 | tf_op jit(solution)/shard_map/all_to_all | solution.py:24
  85.5 3.4 %all-to-all-start.5 = ((bf16[8,64,128]{2,1,0:T(8,128)(2,1)}), bf16[8,64,128]{2,1,0:T(8,128)(2,1)S(1)}, u32[]{:S(2)}, u32[]{:S(2)}) async-start(bf16[8,64,128]{2,1,0:T(8,128)(2,1)} %shard_map.167), calls=%async_computation.5 | async-start | bytes 262144 | tf_op jit(solution)/shard_map/all_to_all | solution.py:24
  90.2 9.4 %shard_map.168.refs_4_.refs_5_.refs_3_ = bf16[6144,128]{1,0:T(8,128)(2,1)} custom-call(s32[1,1024]{1,0:T(1,128)} %constant_dynamic-slice_fusion.1.list_ref, bf16[128,7168]{1,0:T(8,128)(2,1)} %bitcast.19), custom_call_target="tpu_custom_call" | custom-call | tf_op jit(solution)/shard_map/pallas_call | solution.py:43
  100.3 3.2 shard_map.169
  103.5 7.2 %all-to-all-start.6 = ((bf16[16,64,128]{2,1,0:T(8,128)(2,1)}), bf16[16,64,128]{2,1,0:T(8,128)(2,1)S(1)}, u32[]{:S(2)}, u32[]{:S(2)}) async-start(bf16[16,64,128]{2,1,0:T(8,128)(2,1)} %get-tuple-element.18), calls=%async_computation.6 | async-start | bytes 524288 | tf_op jit(solution)/shard_map/all_to_all | solution.py:24
  111.4 8.2 %all-to-all-done.6.refs_0_ = bf16[16,64,128]{2,1,0:T(8,128)(2,1)S(1)} async-done(((bf16[16,64,128]{2,1,0:T(8,128)(2,1)}), bf16[16,64,128]{2,1,0:T(8,128)(2,1)S(1)}, u32[]{:S(2)}, u32[]{:S(2)}) %all-to-all-start.6) | async-done | bytes 262176 | tf_op jit(solution)/shard_map/all_to_all | solution.py:24
  122.0 13.1 %all_to_all.101.refs_0_ = bf16[16,64,128]{2,1,0:T(8,128)(2,1)} all-to-all(bf16[16,64,128]{2,1,0:T(8,128)(2,1)} %shard_map.170), channel_id=1, replica_groups=mesh['ya'=2,'yb'=2,'yc'=2,'x'=4,'c'=2,'z'=8] {'yb','yc','x'}, dimensions={0} | all-to-all | bytes 524288 | tf_op jit(solution)/shard_map/all_to_all | solution.py:24
  136.0 3.5 %all-to-all-start.10 = ((bf16[8,8,4096]{2,1,0:T(8,128)(2,1)}), bf16[8,8,4096]{2,1,0:T(8,128)(2,1)S(1)}, u32[]{:S(2)}, u32[]{:S(2)}) async-start(bf16[8,8,4096]{2,1,0:T(8,128)(2,1)} %broadcast_in_dim.36), calls=%async_computation.10 | async-start | bytes 1048576 | tf_op jit(solution)/shard_map/all_to_all | solution.py:24
  140.1 9.1 %shard_map.171.refs_6_.refs_2_ = bf16[4096,128]{1,0:T(8,128)(2,1)} custom-call(s32[1,2048]{1,0:T(1,128)} %constant_dynamic-slice_fusion.list_ref, bf16[128,7168]{1,0:T(8,128)(2,1)} %bitcast.21), custom_call_target="tpu_custom_call" | custom-call | tf_op jit(solution)/shard_map/pallas_call | solution.py:43
  149.2 5.4 %shard_map.172 = (bf16[64,128]{1,0:T(8,128)(2,1)}, bf16[32,64,128]{2,1,0:T(8,128)(2,1)}) custom-call(bf16[16,64,128]{2,1,0:T(8,128)(2,1)} %all_to_all.101.refs_0_, bf16[128,7168]{1,0:T(8,128)(2,1)} %bitcast.22, bf16[64,128]{1,0:T(8,128)(2,1)} %get-tuple-element.17.refs_2_.refs_3_, bf16[64,128]{1,0:T(8,128)(2,1)} %get-tuple-element.19.refs_3_.refs_2_, ...), custom_call_target="tpu_custom_call" | custom-call | tf_op jit(solution)/shard_map/pallas_call | solution.py:43
  154.6 4.5 %all-to-all-start.8 = ((bf16[32,64,128]{2,1,0:T(8,128)(2,1)}), bf16[32,64,128]{2,1,0:T(8,128)(2,1)S(1)}, u32[]{:S(2)}, u32[]{:S(2)}) async-start(bf16[32,64,128]{2,1,0:T(8,128)(2,1)} %get-tuple-element.20), calls=%async_computation.8 | async-start | bytes 1048576 | tf_op jit(solution)/shard_map/all_to_all | solution.py:24
  159.9 12.1 %all-to-all-done.8.refs_0_ = bf16[32,64,128]{2,1,0:T(8,128)(2,1)S(1)} async-done(((bf16[32,64,128]{2,1,0:T(8,128)(2,1)}), bf16[32,64,128]{2,1,0:T(8,128)(2,1)S(1)}, u32[]{:S(2)}, u32[]{:S(2)}) %all-to-all-start.8) | async-done | bytes 524320 | tf_op jit(solution)/shard_map/all_to_all | solution.py:24
  173.1 10.1 %all-to-all-start.11 = ((bf16[2,64,4096]{2,1,0:T(8,128)(2,1)}), bf16[2,64,4096]{2,1,0:T(8,128)(2,1)S(1)}, u32[]{:S(2)}, u32[]{:S(2)}) async-start(bf16[2,64,4096]{2,1,0:T(8,128)(2,1)} %broadcast_in_dim.38), calls=%async_computation.11 | async-start | bytes 2097152 | tf_op jit(solution)/shard_map/all_to_all | solution.py:24
  185.2 21.4 %all_to_all.102.full_ref = bf16[32,64,128]{2,1,0:T(8,128)(2,1)} all-to-all(bf16[32,64,128]{2,1,0:T(8,128)(2,1)} %shard_map.173), channel_id=1, replica_groups=mesh['ya'=2,'yb'=2,'yc'=2,'x'=4,'c'=2,'z'=8] {'ya','yb','yc','x'}, dimensions={0} | all-to-all | bytes 1048576 | tf_op jit(solution)/shard_map/all_to_all | solution.py:24
  206.6 3.6 %shard_map.174 = bf16[32,64,128]{2,1,0:T(8,128)(2,1)} custom-call(bf16[32,64,128]{2,1,0:T(8,128)(2,1)} %all_to_all.102.full_ref, bf16[128,4096]{1,0:T(8,128)(2,1)} %bitcast.26), custom_call_target="tpu_custom_call" | custom-call | tf_op jit(solution)/shard_map/pallas_call | solution.py:43
  210.2 20.5 %all_to_all.103.refs_0_ = bf16[32,64,128]{2,1,0:T(8,128)(2,1)} all-to-all(bf16[32,64,128]{2,1,0:T(8,128)(2,1)} %shard_map.174), channel_id=1, replica_groups=mesh['ya'=2,'yb'=2,'yc'=2,'x'=4,'c'=2,'z'=8] {'ya','yb','yc','x'}, dimensions={0} | all-to-all | bytes 1048576 | tf_op jit(solution)/shard_map/all_to_all | solution.py:24
  232.7 21.5 %all_to_all.104.refs_0_ = bf16[32,64,128]{2,1,0:T(8,128)(2,1)} all-to-all(bf16[32,64,128]{2,1,0:T(8,128)(2,1)} %get-tuple-element.22), channel_id=1, replica_groups=mesh['ya'=2,'yb'=2,'yc'=2,'x'=4,'c'=2,'z'=8] {'ya','yb','yc','x'}, dimensions={0} | all-to-all | bytes 1048576 | tf_op jit(solution)/shard_map/all_to_all | solution.py:24
  256.9 14.0 %all_to_all.105.refs_0_ = bf16[16,64,128]{2,1,0:T(8,128)(2,1)} all-to-all(bf16[16,64,128]{2,1,0:T(8,128)(2,1)} %shard_map.176), channel_id=1, replica_groups=mesh['ya'=2,'yb'=2,'yc'=2,'x'=4,'c'=2,'z'=8] {'yb','yc','x'}, dimensions={0} | all-to-all | bytes 524288 | tf_op jit(solution)/shard_map/all_to_all | solution.py:24
  272.6 13.0 %all_to_all.106.refs_1_ = bf16[16,64,128]{2,1,0:T(8,128)(2,1)} all-to-all(bf16[16,64,128]{2,1,0:T(8,128)(2,1)} %get-tuple-element.25), channel_id=1, replica_groups=mesh['ya'=2,'yb'=2,'yc'=2,'x'=4,'c'=2,'z'=8] {'yb','yc','x'}, dimensions={0} | all-to-all | bytes 524288 | tf_op jit(solution)/shard_map/all_to_all | solution.py:24
  288.6 9.4 %all_to_all.107.refs_0_ = bf16[8,64,128]{2,1,0:T(8,128)(2,1)} all-to-all(bf16[8,64,128]{2,1,0:T(8,128)(2,1)} %shard_map.178), channel_id=1, replica_groups=mesh['ya'=2,'yb'=2,'yc'=2,'x'=4,'c'=2,'z'=8] {'yc','x'}, dimensions={0} | all-to-all | bytes 262144 | tf_op jit(solution)/shard_map/all_to_all | solution.py:24
  299.6 3.4 %all-to-all-start.17 = ((bf16[8,64,128]{2,1,0:T(8,128)(2,1)}), bf16[8,64,128]{2,1,0:T(8,128)(2,1)S(1)}, u32[]{:S(2)}, u32[]{:S(2)}) async-start(bf16[8,64,128]{2,1,0:T(8,128)(2,1)} %get-tuple-element.27), calls=%async_computation.17 | async-start | bytes 262144 | tf_op jit(solution)/shard_map/all_to_all | solution.py:24
  303.1 5.2 %all-to-all-done.17.refs_2_ = bf16[8,64,128]{2,1,0:T(8,128)(2,1)S(1)} async-done(((bf16[8,64,128]{2,1,0:T(8,128)(2,1)}), bf16[8,64,128]{2,1,0:T(8,128)(2,1)S(1)}, u32[]{:S(2)}, u32[]{:S(2)}) %all-to-all-start.17) | async-done | bytes 131104 | tf_op jit(solution)/shard_map/all_to_all | solution.py:24
  312.0 3.3 all-to-all-start.18
  315.4 4.4 %all-to-all-done.18.refs_0_ = bf16[4,64,128]{2,1,0:T(8,128)(2,1)S(1)} async-done(((bf16[4,64,128]{2,1,0:T(8,128)(2,1)}), bf16[4,64,128]{2,1,0:T(8,128)(2,1)S(1)}, u32[]{:S(2)}, u32[]{:S(2)}) %all-to-all-start.18) | async-done | bytes 65568 | tf_op jit(solution)/shard_map/all_to_all | solution.py:24
  322.9 11.8 %all_to_all.108 = bf16[2,64,256]{2,1,0:T(8,128)(2,1)S(1)} all-to-all(bf16[2,64,256]{2,1,0:T(8,128)(2,1)S(1)} %pad_maximum_fusion), channel_id=1, replica_groups=mesh['ya'=2,'yb'=2,'yc'=2,'x'=4,'c'=2,'z'=8] {'c'}, dimensions={0} | all-to-all | bytes 131072 | tf_op jit(solution)/shard_map/all_to_all | solution.py:24
  (73 shorter events, 44.0 us)
Async XLA Ops:
  0.6 138.8 %copy-start = (s32[2,2048]{1,0:T(2,128)S(1)}, s32[2,2048]{1,0:T(2,128)}, u32[]{:S(2)}) copy-start(s32[2,2048]{1,0:T(2,128)} %param.25) | copy-start | bytes 49156
  2.2 14.5 %all-to-all-start = ((bf16[2,64,256]{2,1,0:T(8,128)(2,1)}), bf16[2,64,256]{2,1,0:T(8,128)(2,1)S(1)}, u32[]{:S(2)}, u32[]{:S(2)}) async-start(bf16[2,64,256]{2,1,0:T(8,128)(2,1)} %bitcast.1), calls=%async_computation | async-start | bytes 131072 | tf_op jit(solution)/shard_map/all_to_all | solution.py:24
  17.6 31.1 %all-to-all-start.2 = ((bf16[8,8,7168]{2,1,0:T(8,128)(2,1)}), bf16[8,8,7168]{2,1,0:T(8,128)(2,1)S(1)}, u32[]{:S(2)}, u32[]{:S(2)}) async-start(bf16[8,8,7168]{2,1,0:T(8,128)(2,1)} %broadcast_in_dim.15), calls=%async_computation.2 | async-start | bytes 1835008 | tf_op jit(solution)/shard_map/all_to_all | solution.py:24
  55.7 14.1 %all-to-all-start.1 = ((bf16[4,64,128]{2,1,0:T(8,128)(2,1)}), bf16[4,64,128]{2,1,0:T(8,128)(2,1)S(1)}, u32[]{:S(2)}, u32[]{:S(2)}) async-start(bf16[4,64,128]{2,1,0:T(8,128)(2,1)} %broadcast_in_dim.14), calls=%async_computation.1 | async-start | bytes 131072 | tf_op jit(solution)/shard_map/all_to_all | solution.py:24
  69.8 0.6 copy-start.7
  72.6 10.7 %all-to-all-start.4 = ((bf16[8,64,128]{2,1,0:T(8,128)(2,1)}), bf16[8,64,128]{2,1,0:T(8,128)(2,1)S(1)}, u32[]{:S(2)}, u32[]{:S(2)}) async-start(bf16[8,64,128]{2,1,0:T(8,128)(2,1)} %get-tuple-element.16), calls=%async_computation.4 | async-start | bytes 262144 | tf_op jit(solution)/shard_map/all_to_all | solution.py:24
  83.3 0.7 copy-start.5
  85.5 14.2 %all-to-all-start.5 = ((bf16[8,64,128]{2,1,0:T(8,128)(2,1)}), bf16[8,64,128]{2,1,0:T(8,128)(2,1)S(1)}, u32[]{:S(2)}, u32[]{:S(2)}) async-start(bf16[8,64,128]{2,1,0:T(8,128)(2,1)} %shard_map.167), calls=%async_computation.5 | async-start | bytes 262144 | tf_op jit(solution)/shard_map/all_to_all | solution.py:24
  99.7 0.6 copy-start.6
  100.3 34.8 %copy-start.9 = (bf16[8,4096]{1,0:T(8,128)(2,1)S(1)}, bf16[8,4096]{1,0:T(8,128)(2,1)}, u32[]{:S(2)}) copy-start(bf16[8,4096]{1,0:T(8,128)(2,1)} %param.18) | copy-start | bytes 196612
  103.5 16.1 %all-to-all-start.6 = ((bf16[16,64,128]{2,1,0:T(8,128)(2,1)}), bf16[16,64,128]{2,1,0:T(8,128)(2,1)S(1)}, u32[]{:S(2)}, u32[]{:S(2)}) async-start(bf16[16,64,128]{2,1,0:T(8,128)(2,1)} %get-tuple-element.18), calls=%async_computation.6 | async-start | bytes 524288 | tf_op jit(solution)/shard_map/all_to_all | solution.py:24
  119.6 0.7 copy-start.3
  136.0 18.7 %all-to-all-start.10 = ((bf16[8,8,4096]{2,1,0:T(8,128)(2,1)}), bf16[8,8,4096]{2,1,0:T(8,128)(2,1)S(1)}, u32[]{:S(2)}, u32[]{:S(2)}) async-start(bf16[8,8,4096]{2,1,0:T(8,128)(2,1)} %broadcast_in_dim.36), calls=%async_computation.10 | async-start | bytes 1048576 | tf_op jit(solution)/shard_map/all_to_all | solution.py:24
  154.6 17.3 %all-to-all-start.8 = ((bf16[32,64,128]{2,1,0:T(8,128)(2,1)}), bf16[32,64,128]{2,1,0:T(8,128)(2,1)S(1)}, u32[]{:S(2)}, u32[]{:S(2)}) async-start(bf16[32,64,128]{2,1,0:T(8,128)(2,1)} %get-tuple-element.20), calls=%async_computation.8 | async-start | bytes 1048576 | tf_op jit(solution)/shard_map/all_to_all | solution.py:24
  172.0 1.1 copy-start.2
  173.1 12.1 %all-to-all-start.11 = ((bf16[2,64,4096]{2,1,0:T(8,128)(2,1)}), bf16[2,64,4096]{2,1,0:T(8,128)(2,1)S(1)}, u32[]{:S(2)}, u32[]{:S(2)}) async-start(bf16[2,64,4096]{2,1,0:T(8,128)(2,1)} %broadcast_in_dim.38), calls=%async_computation.11 | async-start | bytes 2097152 | tf_op jit(solution)/shard_map/all_to_all | solution.py:24
  185.2 21.4 %copy-start.1 = (bf16[2,64,4096]{2,1,0:T(8,128)(2,1)}, bf16[2,64,4096]{2,1,0:T(8,128)(2,1)S(1)}, u32[]{:S(2)}) copy-start(bf16[2,64,4096]{2,1,0:T(8,128)(2,1)S(1)} %all-to-all-done.11) | copy-start | bytes 3145732
  285.7 17.3 %copy-start.11 = (bf16[64,128]{1,0:T(8,128)(2,1)S(1)}, bf16[64,128]{1,0:T(8,128)(2,1)}, u32[]{:S(2)}) copy-start(bf16[64,128]{1,0:T(8,128)(2,1)} %get-tuple-element.21) | copy-start | bytes 49156
  285.7 17.4 %copy-start.12 = (bf16[64,128]{1,0:T(8,128)(2,1)S(1)}, bf16[64,128]{1,0:T(8,128)(2,1)}, u32[]{:S(2)}) copy-start(bf16[64,128]{1,0:T(8,128)(2,1)} %get-tuple-element.24) | copy-start | bytes 49156
  299.6 8.7 %all-to-all-start.17 = ((bf16[8,64,128]{2,1,0:T(8,128)(2,1)}), bf16[8,64,128]{2,1,0:T(8,128)(2,1)S(1)}, u32[]{:S(2)}, u32[]{:S(2)}) async-start(bf16[8,64,128]{2,1,0:T(8,128)(2,1)} %get-tuple-element.27), calls=%async_computation.17 | async-start | bytes 262144 | tf_op jit(solution)/shard_map/all_to_all | solution.py:24
  303.1 12.2 %copy-start.10 = (bf16[64,128]{1,0:T(8,128)(2,1)S(1)}, bf16[64,128]{1,0:T(8,128)(2,1)}, u32[]{:S(2)}) copy-start(bf16[64,128]{1,0:T(8,128)(2,1)} %get-tuple-element.26) | copy-start | bytes 49156
  308.3 0.6 copy-start.4
  312.0 7.7 %all-to-all-start.18 = ((bf16[4,64,128]{2,1,0:T(8,128)(2,1)}), bf16[4,64,128]{2,1,0:T(8,128)(2,1)S(1)}, u32[]{:S(2)}, u32[]{:S(2)}) async-start(bf16[4,64,128]{2,1,0:T(8,128)(2,1)} %shard_map.180), calls=%async_computation.18 | async-start | bytes 131072 | tf_op jit(solution)/shard_map/all_to_all | solution.py:24
  319.8 0.6 copy-start.8

commit v2 on v1

v2 whole, which is shorter than its diff:
```python
import functools

import jax
import jax.numpy as jnp
from jax import lax
from jax.experimental import pallas as pl
from jax.sharding import Mesh
from jax.sharding import PartitionSpec as P

LEVELS = 4
BLOCK = 128
HALF = 64
CHUNK = 256
INTERPRET = False

CHIPS = ("ya", "yb", "yc", "x")
GROUP_AXES = (CHIPS, CHIPS[1:], CHIPS[2:], CHIPS[3:])
GROUP_SIZE = (32, 16, 8, 4)
COLUMN = ("ya", "yb", "yc")
LEAF = ("ya", "yb", "yc", "x", "c")


def exchange(value, axes):
    return lax.all_to_all(value, axes, 0, 0, tiled=True)


def dot_nt(left, right):
    return lax.dot_general(left, right, (((1,), (1,)), ((), ())), preferred_element_type=jnp.float32)


def dot_nn(left, right):
    return lax.dot_general(left, right, (((1,), (0,)), ((), ())), preferred_element_type=jnp.float32)


def call(kernel, out_shapes, inputs):
    specs = []
    arrays = []
    for item in inputs:
        array, shape, index = item if isinstance(item, tuple) else (item, item.shape, (0,) * item.ndim)
        specs.append(pl.BlockSpec(shape, functools.partial(lambda at, _: at, index)))
        arrays.append(array)
    out_specs = [pl.BlockSpec(o.shape, functools.partial(lambda at, _: at, (0,) * len(o.shape))) for o in out_shapes]
    return pl.pallas_call(
        kernel, grid=(1,), in_specs=specs, out_specs=out_specs, out_shape=out_shapes, interpret=INTERPRET
    )(*arrays)


def bf16(*shape):
    return jax.ShapeDtypeStruct(shape, jnp.bfloat16)


def expand_kernel(base, list_ref, first_ref, second_ref, out_ref):
    block = jnp.concatenate([first_ref[...], second_ref[...]], axis=0)
    rows = list_ref[...] - base
    width = block.shape[1]
    lane = lax.broadcasted_iota(jnp.int32, (CHUNK, width), 0).astype(jnp.float32).astype(jnp.bfloat16)

    def step(at, carry):
        shifted = jnp.clip(rows - at * CHUNK, -1, CHUNK).astype(jnp.float32).astype(jnp.bfloat16)
        hit = jnp.where(shifted == lane, jnp.bfloat16(1), jnp.bfloat16(0))
        out_ref[pl.ds(pl.multiple_of(at * CHUNK, CHUNK), CHUNK), :] = dot_nt(hit, block).astype(jnp.bfloat16)
        return carry

    lax.fori_loop(0, out_ref.shape[0] // CHUNK, step, 0, unroll=4)


def expanded(row_list, pieces, base, count):
    kernel = functools.partial(expand_kernel, base)
    return call(kernel, [bf16(count, BLOCK)], [row_list] + pieces)[0]


def pairs_product(full_ref, weights, count):
    total = None
    for at in range(0, count, 2):
        left = jnp.concatenate([full_ref[at], full_ref[at + 1]], axis=1)
        part = weights(left, at)
        total = part if total is None else total + part
    return total


def front_values(full_ref, inverse, count, first=0):
    return pairs_product(
        full_ref, lambda left, at: dot_nt(left, inverse[:, first + at * BLOCK : first + (at + 2) * BLOCK]), count
    )


def forward_kernel(deeper, count, send_count, *refs):
    full_ref, first_ref, second_ref = refs[:3]
    old = refs[3 : 3 + deeper]
    couplings = refs[3 + deeper : 4 + 2 * deeper]
    values_ref, send_ref = refs[-2:]
    inverse = jnp.concatenate([first_ref[...], second_ref[...]], axis=0)
    values = front_values(full_ref, inverse, count).astype(jnp.bfloat16)
    values_ref[...] = values
    stacked = [r[...] for r in old] + [values]
    for at in range(send_count):
        total = None
        for left, ref in zip(stacked, couplings):
            part = dot_nt(left, ref[at * BLOCK : (at + 1) * BLOCK, :])
            total = part if total is None else total + part
        send_ref[at] = total.astype(jnp.bfloat16)


def spread_kernel(count, has_own, *refs):
    parts_ref = refs[0]
    total = refs[1][...].astype(jnp.float32) if has_own else None
    for at in range(count):
        part = parts_ref[at].astype(jnp.float32)
        total = part if total is None else total + part
    result = total.astype(jnp.bfloat16)
    for out_ref in refs[1 + has_own :]:
        if len(out_ref.shape) == 2:
            out_ref[...] = result
        else:
            for at in range(out_ref.shape[0]):
                out_ref[at] = result


def root_values_kernel(full_ref, first_ref, second_ref, send_ref):
    inverse = jnp.concatenate([first_ref[...], second_ref[...]], axis=0)
    for part in range(4):
        partial = front_values(full_ref, inverse, 8, part * 8 * BLOCK).astype(jnp.bfloat16)
        for at in range(4):
            send_ref[at, :, part * BLOCK : (part + 1) * BLOCK] = partial


def root_solve_kernel(parts_ref, first_ref, second_ref, send_ref):
    inverse = jnp.concatenate([first_ref[...], second_ref[...]], axis=0)
    total = parts_ref[0].astype(jnp.float32)
    for at in range(1, 4):
        total = total + parts_ref[at].astype(jnp.float32)
    values = total.astype(jnp.bfloat16)
    for at in range(8):
        solved = None
        for part in range(4):
            start = (part * 8 + at) * BLOCK
            piece = dot_nn(values[:, part * BLOCK : (part + 1) * BLOCK], inverse[:, start : start + BLOCK])
            solved = piece if solved is None else solved + piece
        send_ref[at] = solved.astype(jnp.bfloat16)


def backward_kernel(depth, *refs):
    solved = refs[:depth]
    values_ref, first_ref, second_ref = refs[depth : depth + 3]
    couplings = refs[depth + 3 : 2 * depth + 3]
    send_ref = refs[-1]
    total = values_ref[...].astype(jnp.float32)
    for upper in range(depth):

        def product(left, at):
            return dot_nn(left, couplings[upper][at * BLOCK : (at + 2) * BLOCK, :])

        total = total - pairs_product(solved[upper], product, GROUP_SIZE[upper])
    adjusted = total.astype(jnp.bfloat16)
    inverse = jnp.concatenate([first_ref[...], second_ref[...]], axis=0)
    for at in range(GROUP_SIZE[depth]):
        send_ref[at] = dot_nn(adjusted, inverse[:, at * BLOCK : (at + 1) * BLOCK]).astype(jnp.bfloat16)


def copies_kernel(*refs):
    out_ref = refs[-1]
    for at in range(out_ref.shape[0]):
        start = 0
        for ref in refs[:-1]:
            width = ref.shape[1]
            out_ref[at, :, start : start + width] = ref[...]
            start += width


def partner(value, axis, mask):
    size = lax.axis_size(axis)
    return lax.ppermute(value, axis, [(at, at ^ mask) for at in range(size)])


def in_order(mine, other, axis):
    low = lax.axis_index("c") == 0
    first = jnp.where(low, mine, other)
    second = jnp.where(low, other, mine)
    return jnp.concatenate([first, second], axis=axis)


def solve(
    rhs_0, rhs_1, rhs_2, rhs_3, inv_0, inv_1, inv_2, inv_3, coupling_1, coupling_2, coupling_3, rows_1, rows_2, rows_3
):
    panels = lax.axis_size("z")
    shard_rows = inv_0.shape[0]
    core = lax.axis_index("c")
    copies = call(copies_kernel, [bf16(panels, shard_rows, 3072)], [inv_2, coupling_2, inv_3, coupling_3])[0]
    low = exchange(copies, "z").reshape(HALF, 3072)
    stacked = jnp.concatenate([rhs_0, rhs_1, rhs_2, rhs_3], axis=0).T
    mine = lax.dynamic_slice_in_dim(stacked, core * HALF, HALF, 0)
    other = partner(lax.dynamic_slice_in_dim(stacked, (1 - core) * HALF, HALF, 0), "c", 1)
    rhs = [in_order(mine[:, k * HALF : (k + 1) * HALF], other[:, k * HALF : (k + 1) * HALF], 1) for k in range(LEVELS)]
    low = [low, partner(low, "c", 1)]
    top = inv_0.reshape(shard_rows, 8, 4, BLOCK).transpose(2, 1, 0, 3).reshape(4, 8 * shard_rows, BLOCK)
    sent = jnp.concatenate([jnp.broadcast_to(rhs[3][None], (4, HALF, BLOCK)), top], axis=1)
    full = exchange(sent, "x")
    top = full[:, HALF:].reshape(32, shard_rows, BLOCK).transpose(1, 0, 2).reshape(shard_rows, 4096)
    high = jnp.concatenate([inv_1, coupling_1, top], axis=1)
    mask = panels // 2
    while mask:
        high = jnp.concatenate([high, partner(high, "z", mask)], axis=0)
        mask //= 2
    high = [high, partner(high, "c", 1)]

    def pieces(arrays, width, at):
        return [(a, (HALF, width), (0, at)) for a in arrays]

    inv = [pieces(high, 4096, 1), pieces(high, 2048, 0), pieces(low, 1024, 0), pieces(low, 512, 4)]
    coup = [None, pieces(high, 2048, 1), pieces(low, 1024, 1), pieces(low, 512, 5)]
    chip = lax.axis_index(CHIPS)
    lists = [None] + [
        lax.dynamic_slice_in_dim(rows, chip // GROUP_SIZE[k], 1, 0)
        for k, rows in ((1, rows_1), (2, rows_2), (3, rows_3))
    ]
    near_3 = expanded(lists[3], coup[3], 6144, 1024)
    near_2 = expanded(lists[2], coup[2], 4096, 2048)
    far_3 = expanded(lists[3], coup[3], 0, 6144)
    far_2 = expanded(lists[2], coup[2], 0, 4096)
    near_1 = expanded(lists[1], coup[1], 0, 4096)
    to_0 = lambda a: (a, (4096, BLOCK), (0, 0))
    far_31 = (far_3, (2048, BLOCK), (2, 0))
    exp = [None, [near_1], [to_0(far_2), near_2], [to_0(far_3), far_31, near_3]]

    values = [None] * LEVELS
    full = (full, (4, HALF, BLOCK), (0, 0, 0))
    for k in (3, 2, 1):
        send_count = GROUP_SIZE[k - 1]
        order = list(range(3, k, -1))
        values[k], parts = call(
            functools.partial(forward_kernel, len(order), GROUP_SIZE[k], send_count),
            [bf16(HALF, BLOCK), bf16(send_count, HALF, BLOCK)],
            [full] + inv[k] + [values[j] for j in order] + [exp[j][k - 1] for j in order + [k]],
        )
        parts = exchange(parts, GROUP_AXES[k - 1])
        spread_count = send_count if k > 1 else 8
        sent = call(
            functools.partial(spread_kernel, send_count, 1), [bf16(spread_count, HALF, BLOCK)], [parts, rhs[k - 1]]
        )[0]
        full = exchange(sent, GROUP_AXES[k - 1] if k > 1 else COLUMN)
    parts = call(root_values_kernel, [bf16(4, HALF, 4 * BLOCK)], [full] + inv[0])[0]
    parts = exchange(parts, "x")
    parts = call(root_solve_kernel, [bf16(8, HALF, BLOCK)], [parts] + inv[0])[0]
    solved = []
    out = []
    for k in range(LEVELS):
        parts = exchange(parts, GROUP_AXES[k] if k else COLUMN)
        kernel = functools.partial(spread_kernel, GROUP_SIZE[k] if k else 8, 0)
        if k == LEVELS - 1:
            out.append(call(kernel, [bf16(HALF, BLOCK)], [parts])[0])
            break
        sent, own = call(kernel, [bf16(GROUP_SIZE[k], HALF, BLOCK), bf16(HALF, BLOCK)], [parts])
        out.append(own)
        solved.append(exchange(sent, GROUP_AXES[k]))
        parts = call(
            functools.partial(backward_kernel, k + 1),
            [bf16(GROUP_SIZE[k + 1], HALF, BLOCK)],
            solved + [values[k + 1]] + inv[k + 1] + exp[k + 1],
        )[0]
    lows = jnp.concatenate([o[:, :HALF] for o in out], axis=1)
    highs = jnp.concatenate([o[:, HALF:] for o in out], axis=1)
    low_core = core == 0
    other = partner(jnp.where(low_core, highs, lows), "c", 1)
    rows = in_order(jnp.where(low_core, lows, highs), other, 0).T
    return tuple(rows[k * HALF : (k + 1) * HALF] for k in range(LEVELS))


def solution(mesh):
    devices = mesh.devices
    fine = Mesh(devices.reshape(2, 2, 2, 4, 2, devices.size // 64), ("ya", "yb", "yc", "x", "c", "z"))
    wide = P(LEAF, "z")
    rows = P(LEAF + ("z",), None)
    return jax.shard_map(
        solve,
        mesh=fine,
        in_specs=(wide,) * 4 + (rows,) * 7 + (P(None, None),) * 3,
        out_specs=(wide,) * 4,
        check_vma=False,
    )
```

time: 338 us -> 314 us (0.929)
  blocking collectives: 131 us -> 93.9 us
  starting transfers between devices: 59.4 us -> 85.6 us
  waiting for transfers between devices: 60.9 us -> 50.5 us
    ppermute x0 -> x7, starting transfers between devices: none -> 48.6 us  [partner(): return lax.ppermute(value, axis, [(at, at ^ mask) for at in range(size)])]
    all_to_all x9 -> x8, blocking collectives: 131 us -> 93.9 us  [exchange(): return lax.all_to_all(value, axes, 0, 0, tiled=True)]
    all_to_all x11 -> x8, starting transfers between devices: 59.4 us -> 37.1 us  [exchange(): return lax.all_to_all(value, axes, 0, 0, tiled=True)]
    all_to_all x11 -> x8, waiting for transfers between devices: 60.9 us -> 46.8 us  [exchange(): return lax.all_to_all(value, axes, 0, 0, tiled=True)]
    unnamed x31 -> x44, local copies, waits for them, and re-layouts: 7.56 us -> 12.7 us
    broadcast_in_dim x5 -> x1, local copies, waits for them, and re-layouts: 3.75 us -> 0.01 us  [solve(): jnp.broadcast_to(rhs[3][None], (4, HALF, BLOCK))]
    ppermute x0 -> x7, waiting for transfers between devices: none -> 3.67 us  [partner(): return lax.ppermute(value, axis, [(at, at ^ mask) for at in range(size)])]
    pallas_call x17 -> x21, Pallas kernels: 62.4 us -> 59.6 us  [call(): pl.pallas_call(kernel, grid=(1,), in_specs=specs, out_specs=out_specs, ou...]
  transfers between devices with their start and end apart: 11 -> 15, of which waited for: 6 -> 8; matrix products, arithmetic and copies ran while one was open for 3% -> 2% of each run, Pallas kernels for 10% -> 10%
where the time goes in v2:
time: 314 us; the launch traced here: 311 us
  blocking collectives  93.9 us (30%)
  starting transfers between devices  85.6 us (27%)
  Pallas kernels  59.6 us (19%)
  waiting for transfers between devices  50.5 us (16%)
  local copies, waits for them, and re-layouts  18 us (6%)
    all_to_all x8, blocking collectives, exchange(): return lax.all_to_all(value, axes, 0, 0, tiled=True)  93.9 us
    pallas_call x21, Pallas kernels, call(): pl.pallas_call(kernel, grid=(1,), in_specs=specs, out_specs=out_specs, ou...  59.6 us
    ppermute x7, starting transfers between devices, partner(): return lax.ppermute(value, axis, [(at, at ^ mask) for at in range(size)])  48.6 us
    all_to_all x8, waiting for transfers between devices, exchange(): return lax.all_to_all(value, axes, 0, 0, tiled=True)  46.8 us
    all_to_all x8, starting transfers between devices, exchange(): return lax.all_to_all(value, axes, 0, 0, tiled=True)  37.1 us
    unnamed x44, local copies, waits for them, and re-layouts  12.7 us
  transfers between devices with their start and end apart: 15, of which 8 were waited for; matrix products, arithmetic and copies ran while one was open for 2% of the time, Pallas kernels for 10%

profile of v2, /device:TPU:1, one launch (start us, length us, event | category | flops | bytes accessed | tf_op | source)
XLA Modules:
  0.0 311.3 jit_solution(13114881928654589775)
XLA Ops:
  4.2 8.7 %collective-permute-start = (bf16[64,256]{1,0:T(8,128)(2,1)S(1)}, bf16[64,256]{1,0:T(8,128)(2,1)S(1)}, u32[]{:S(2)}, u32[]{:S(2)}) collective-permute-start(bf16[64,256]{1,0:T(8,128)(2,1)S(1)} %get-tuple-element.47), channel_id=1, source_target_pairs={{0,8},{8,0},{1,9},{9,1},{2,10},{10,2},{3,11},{11,3},{4,12},{12,4},... | collective-permute-start | bytes 98312 | tf_op jit(solution)/shard_map/ppermute | solution.py:172
  14.0 7.2 %all_to_all.80.refs_0_ = bf16[4,128,128]{2,1,0:T(8,128)(2,1)S(1)} all-to-all(bf16[4,128,128]{2,1,0:T(8,128)(2,1)S(1)} %pad_maximum_fusion.3), channel_id=1, replica_groups=mesh['ya'=2,'yb'=2,'yc'=2,'x'=4,'c'=2,'z'=8] {'x'}, dimensions={0} | all-to-all | bytes 262144 | tf_op jit(solution)/shard_map/all_to_all | solution.py:24
  21.3 6.7 %collective-permute-start.2 = (bf16[8,8192]{1,0:T(8,128)(2,1)S(1)}, bf16[8,8192]{1,0:T(8,128)(2,1)S(1)}, u32[]{:S(2)}, u32[]{:S(2)}) collective-permute-start(bf16[8,8192]{1,0:T(8,128)(2,1)S(1)} %pad_maximum_fusion.4), channel_id=1, source_target_pairs={{0,4},{1,5},{2,6},{3,7},{4,0},{5,1},{6,2},{7,3},{8,12},{9,13},{10,... | collective-permute-start | bytes 393224 | tf_op jit(solution)/shard_map/ppermute | solution.py:172
  29.5 4.3 %all-to-all-start.1 = ((bf16[8,8,3072]{2,1,0:T(8,128)(2,1)}), bf16[8,8,3072]{2,1,0:T(8,128)(2,1)S(1)}, u32[]{:S(2)}, u32[]{:S(2)}) async-start(bf16[8,8,3072]{2,1,0:T(8,128)(2,1)} %shard_map.165), calls=%async_computation.1 | async-start | bytes 786432 | tf_op jit(solution)/shard_map/all_to_all | solution.py:24
  33.8 4.4 %collective-permute-start.3 = (bf16[16,8192]{1,0:T(8,128)(2,1)S(1)}, bf16[16,8192]{1,0:T(8,128)(2,1)S(1)}, u32[]{:S(2)}, u32[]{:S(2)}) collective-permute-start(bf16[16,8192]{1,0:T(8,128)(2,1)S(1)} %pad_maximum_fusion.2), channel_id=1, source_target_pairs={{0,2},{1,3},{2,0},{3,1},{4,6},{5,7},{6,4},{7,5},{8,10},{9,11},{10,... | collective-permute-start | bytes 786440 | tf_op jit(solution)/shard_map/ppermute | solution.py:172
  38.2 7.8 %all-to-all-done.1 = bf16[8,8,3072]{2,1,0:T(8,128)(2,1)S(1)} async-done(((bf16[8,8,3072]{2,1,0:T(8,128)(2,1)}), bf16[8,8,3072]{2,1,0:T(8,128)(2,1)S(1)}, u32[]{:S(2)}, u32[]{:S(2)}) %all-to-all-start.1) | async-done | bytes 393248 | tf_op jit(solution)/shard_map/all_to_all | solution.py:24
  46.0 6.9 %collective-permute-start.1 = (bf16[64,3072]{1,0:T(8,128)(2,1)S(1)}, bf16[64,3072]{1,0:T(8,128)(2,1)S(1)}, u32[]{:S(2)}, u32[]{:S(2)}) collective-permute-start(bf16[64,3072]{1,0:T(8,128)(2,1)S(1)} %bitcast.18), channel_id=1, source_target_pairs={{0,8},{8,0},{1,9},{9,1},{2,10},{10,2},{3,11},{11,3},{4,12},{12,4},... | collective-permute-start | bytes 1179656 | tf_op jit(solution)/shard_map/ppermute | solution.py:172
  64.1 3.4 %all-to-all-start.2 = ((bf16[8,64,128]{2,1,0:T(8,128)(2,1)}), bf16[8,64,128]{2,1,0:T(8,128)(2,1)S(1)}, u32[]{:S(2)}, u32[]{:S(2)}) async-start(bf16[8,64,128]{2,1,0:T(8,128)(2,1)} %get-tuple-element.16), calls=%async_computation.2 | async-start | bytes 262144 | tf_op jit(solution)/shard_map/all_to_all | solution.py:24
  68.2 4.7 %all-to-all-done.2.refs_0_ = bf16[8,64,128]{2,1,0:T(8,128)(2,1)S(1)} async-done(((bf16[8,64,128]{2,1,0:T(8,128)(2,1)}), bf16[8,64,128]{2,1,0:T(8,128)(2,1)S(1)}, u32[]{:S(2)}, u32[]{:S(2)}) %all-to-all-start.2) | async-done | bytes 131104 | tf_op jit(solution)/shard_map/all_to_all | solution.py:24
  75.1 3.4 %all-to-all-start.3 = ((bf16[8,64,128]{2,1,0:T(8,128)(2,1)}), bf16[8,64,128]{2,1,0:T(8,128)(2,1)S(1)}, u32[]{:S(2)}, u32[]{:S(2)}) async-start(bf16[8,64,128]{2,1,0:T(8,128)(2,1)} %shard_map.168), calls=%async_computation.3 | async-start | bytes 262144 | tf_op jit(solution)/shard_map/all_to_all | solution.py:24
  78.6 5.1 %collective-permute-start.5 = (bf16[64,8192]{1,0:T(8,128)(2,1)S(1)}, bf16[64,8192]{1,0:T(8,128)(2,1)S(1)}, u32[]{:S(2)}, u32[]{:S(2)}) collective-permute-start(bf16[64,8192]{1,0:T(8,128)(2,1)S(1)} %pad_maximum_fusion.first_ref.refs_1_.refs_2_), channel_id=1, source_target_pairs={{0,8},{8,0},{1,9},{9,1},{2,10},{10,2},{3,11},{11,3},{4,12},{12,4},... | collective-permute-start | bytes 3145736 | tf_op jit(solution)/shard_map/ppermute | solution.py:172
  85.0 4.7 %shard_map.169.refs_4_.refs_5_.refs_6_.refs_7_ = bf16[6144,128]{1,0:T(8,128)(2,1)} custom-call(s32[1,512]{1,0:T(1,128)} %constant_dynamic-slice_fusion.2.list_ref, bf16[64,3072]{1,0:T(8,128)(2,1)} %bitcast.21, bf16[64,3072]{1,0:T(8,128)(2,1)} %copy-done.4), custom_call_target="tpu_custom_call" | custom-call | tf_op jit(solution)/shard_map/pallas_call | solution.py:43
  96.8 7.5 %all-to-all-start.4 = ((bf16[16,64,128]{2,1,0:T(8,128)(2,1)}), bf16[16,64,128]{2,1,0:T(8,128)(2,1)S(1)}, u32[]{:S(2)}, u32[]{:S(2)}) async-start(bf16[16,64,128]{2,1,0:T(8,128)(2,1)} %get-tuple-element.18), calls=%async_computation.4 | async-start | bytes 524288 | tf_op jit(solution)/shard_map/all_to_all | solution.py:24
  105.0 9.5 %all-to-all-done.4.refs_0_ = bf16[16,64,128]{2,1,0:T(8,128)(2,1)S(1)} async-done(((bf16[16,64,128]{2,1,0:T(8,128)(2,1)}), bf16[16,64,128]{2,1,0:T(8,128)(2,1)S(1)}, u32[]{:S(2)}, u32[]{:S(2)}) %all-to-all-start.4) | async-done | bytes 262176 | tf_op jit(solution)/shard_map/all_to_all | solution.py:24
  116.9 4.1 %all-to-all-start.5 = ((bf16[16,64,128]{2,1,0:T(8,128)(2,1)}), bf16[16,64,128]{2,1,0:T(8,128)(2,1)S(1)}, u32[]{:S(2)}, u32[]{:S(2)}) async-start(bf16[16,64,128]{2,1,0:T(8,128)(2,1)} %shard_map.172), calls=%async_computation.5 | async-start | bytes 524288 | tf_op jit(solution)/shard_map/all_to_all | solution.py:24
  121.6 4.8 %shard_map.173.refs_6_.refs_5_ = bf16[4096,128]{1,0:T(8,128)(2,1)} custom-call(s32[1,1024]{1,0:T(1,128)} %constant_dynamic-slice_fusion.1.list_ref, bf16[64,3072]{1,0:T(8,128)(2,1)} %bitcast.24, bf16[64,3072]{1,0:T(8,128)(2,1)} %copy-done.4), custom_call_target="tpu_custom_call" | custom-call | tf_op jit(solution)/shard_map/pallas_call | solution.py:43
  127.5 7.1 %shard_map.174.refs_7_.refs_4_ = bf16[4096,128]{1,0:T(8,128)(2,1)} custom-call(s32[1,2048]{1,0:T(1,128)} %constant_dynamic-slice_fusion.list_ref, bf16[64,8192]{1,0:T(8,128)(2,1)} %copy-done.1, bf16[64,8192]{1,0:T(8,128)(2,1)} %copy-done.3), custom_call_target="tpu_custom_call" | custom-call | tf_op jit(solution)/shard_map/pallas_call | solution.py:43
  135.3 5.4 %shard_map.175 = (bf16[64,128]{1,0:T(8,128)(2,1)}, bf16[32,64,128]{2,1,0:T(8,128)(2,1)}) custom-call(bf16[16,64,128]{2,1,0:T(8,128)(2,1)} %copy-done.6, bf16[64,8192]{1,0:T(8,128)(2,1)} %copy-done.1, bf16[64,8192]{1,0:T(8,128)(2,1)} %copy-done.3, bf16[64,128]{1,0:T(8,128)(2,1)} %get-tuple-element.17.refs_3_, ...), custom_call_target="tpu_custom_call" | custom-call | tf_op jit(solution)/shard_map/pallas_call | solution.py:43
  140.7 7.8 %all-to-all-start.6 = ((bf16[32,64,128]{2,1,0:T(8,128)(2,1)}), bf16[32,64,128]{2,1,0:T(8,128)(2,1)S(1)}, u32[]{:S(2)}, u32[]{:S(2)}) async-start(bf16[32,64,128]{2,1,0:T(8,128)(2,1)} %get-tuple-element.20), calls=%async_computation.6 | async-start | bytes 1048576 | tf_op jit(solution)/shard_map/all_to_all | solution.py:24
  149.2 14.7 %all-to-all-done.6.refs_0_ = bf16[32,64,128]{2,1,0:T(8,128)(2,1)S(1)} async-done(((bf16[32,64,128]{2,1,0:T(8,128)(2,1)}), bf16[32,64,128]{2,1,0:T(8,128)(2,1)S(1)}, u32[]{:S(2)}, u32[]{:S(2)}) %all-to-all-start.6) | async-done | bytes 524320 | tf_op jit(solution)/shard_map/all_to_all | solution.py:24
  166.5 12.0 %all_to_all.81.full_ref = bf16[8,64,128]{2,1,0:T(8,128)(2,1)} all-to-all(bf16[8,64,128]{2,1,0:T(8,128)(2,1)} %shard_map.176), channel_id=1, replica_groups=mesh['ya'=2,'yb'=2,'yc'=2,'x'=4,'c'=2,'z'=8] {'ya','yb','yc'}, dimensions={0} | all-to-all | bytes 262144 | tf_op jit(solution)/shard_map/all_to_all | solution.py:24
  181.0 9.8 %all_to_all.82.parts_ref = bf16[4,64,512]{2,1,0:T(8,128)(2,1)} all-to-all(bf16[4,64,512]{2,1,0:T(8,128)(2,1)} %shard_map.177), channel_id=1, replica_groups=mesh['ya'=2,'yb'=2,'yc'=2,'x'=4,'c'=2,'z'=8] {'x'}, dimensions={0} | all-to-all | bytes 524288 | tf_op jit(solution)/shard_map/all_to_all | solution.py:24
  193.1 11.9 %all_to_all.83.refs_0_ = bf16[8,64,128]{2,1,0:T(8,128)(2,1)} all-to-all(bf16[8,64,128]{2,1,0:T(8,128)(2,1)} %shard_map.178), channel_id=1, replica_groups=mesh['ya'=2,'yb'=2,'yc'=2,'x'=4,'c'=2,'z'=8] {'ya','yb','yc'}, dimensions={0} | all-to-all | bytes 262144 | tf_op jit(solution)/shard_map/all_to_all | solution.py:24
  206.8 17.5 %all_to_all.84.refs_0_ = bf16[32,64,128]{2,1,0:T(8,128)(2,1)} all-to-all(bf16[32,64,128]{2,1,0:T(8,128)(2,1)} %get-tuple-element.22), channel_id=1, replica_groups=mesh['ya'=2,'yb'=2,'yc'=2,'x'=4,'c'=2,'z'=8] {'ya','yb','yc','x'}, dimensions={0} | all-to-all | bytes 1048576 | tf_op jit(solution)/shard_map/all_to_all | solution.py:24
  227.1 13.0 %all_to_all.85.refs_0_ = bf16[16,64,128]{2,1,0:T(8,128)(2,1)} all-to-all(bf16[16,64,128]{2,1,0:T(8,128)(2,1)} %shard_map.180), channel_id=1, replica_groups=mesh['ya'=2,'yb'=2,'yc'=2,'x'=4,'c'=2,'z'=8] {'yb','yc','x'}, dimensions={0} | all-to-all | bytes 524288 | tf_op jit(solution)/shard_map/all_to_all | solution.py:24
  241.9 13.0 %all_to_all.86.refs_1_ = bf16[16,64,128]{2,1,0:T(8,128)(2,1)} all-to-all(bf16[16,64,128]{2,1,0:T(8,128)(2,1)} %get-tuple-element.25), channel_id=1, replica_groups=mesh['ya'=2,'yb'=2,'yc'=2,'x'=4,'c'=2,'z'=8] {'yb','yc','x'}, dimensions={0} | all-to-all | bytes 524288 | tf_op jit(solution)/shard_map/all_to_all | solution.py:24
  257.9 9.4 %all_to_all.87.refs_0_ = bf16[8,64,128]{2,1,0:T(8,128)(2,1)} all-to-all(bf16[8,64,128]{2,1,0:T(8,128)(2,1)} %shard_map.182), channel_id=1, replica_groups=mesh['ya'=2,'yb'=2,'yc'=2,'x'=4,'c'=2,'z'=8] {'yc','x'}, dimensions={0} | all-to-all | bytes 262144 | tf_op jit(solution)/shard_map/all_to_all | solution.py:24
  268.9 3.4 %all-to-all-start.14 = ((bf16[8,64,128]{2,1,0:T(8,128)(2,1)}), bf16[8,64,128]{2,1,0:T(8,128)(2,1)S(1)}, u32[]{:S(2)}, u32[]{:S(2)}) async-start(bf16[8,64,128]{2,1,0:T(8,128)(2,1)} %get-tuple-element.27), calls=%async_computation.14 | async-start | bytes 262144 | tf_op jit(solution)/shard_map/all_to_all | solution.py:24
  272.5 5.5 %all-to-all-done.14.refs_2_ = bf16[8,64,128]{2,1,0:T(8,128)(2,1)S(1)} async-done(((bf16[8,64,128]{2,1,0:T(8,128)(2,1)}), bf16[8,64,128]{2,1,0:T(8,128)(2,1)S(1)}, u32[]{:S(2)}, u32[]{:S(2)}) %all-to-all-start.14) | async-done | bytes 131104 | tf_op jit(solution)/shard_map/all_to_all | solution.py:24
  281.7 3.3 %all-to-all-start.15 = ((bf16[4,64,128]{2,1,0:T(8,128)(2,1)}), bf16[4,64,128]{2,1,0:T(8,128)(2,1)S(1)}, u32[]{:S(2)}, u32[]{:S(2)}) async-start(bf16[4,64,128]{2,1,0:T(8,128)(2,1)} %shard_map.184), calls=%async_computation.15 | async-start | bytes 131072 | tf_op jit(solution)/shard_map/all_to_all | solution.py:24
  285.1 4.6 %all-to-all-done.15.refs_0_ = bf16[4,64,128]{2,1,0:T(8,128)(2,1)S(1)} async-done(((bf16[4,64,128]{2,1,0:T(8,128)(2,1)}), bf16[4,64,128]{2,1,0:T(8,128)(2,1)S(1)}, u32[]{:S(2)}, u32[]{:S(2)}) %all-to-all-start.15) | async-done | bytes 65568 | tf_op jit(solution)/shard_map/all_to_all | solution.py:24
  292.7 14.8 %collective-permute-start.6 = (bf16[64,256]{1,0:T(8,128)(2,1)S(1)}, bf16[64,256]{1,0:T(8,128)(2,1)S(1)}, u32[]{:S(2)}, u32[]{:S(2)}) collective-permute-start(bf16[64,256]{1,0:T(8,128)(2,1)S(1)} %broadcast_select_fusion.2), channel_id=1, source_target_pairs={{0,8},{8,0},{1,9},{9,1},{2,10},{10,2},{3,11},{11,3},{4,12},{12,4},... | collective-permute-start | bytes 98312 | tf_op jit(solution)/shard_map/ppermute | solution.py:172
  (97 shorter events, 63.8 us)
Async XLA Ops:
  0.6 120.4 %copy-start = (s32[2,2048]{1,0:T(2,128)S(1)}, s32[2,2048]{1,0:T(2,128)}, u32[]{:S(2)}) copy-start(s32[2,2048]{1,0:T(2,128)} %param.25) | copy-start | bytes 49156
  0.6 20.6 %copy-start.9 = (bf16[8,2048]{1,0:T(8,128)(2,1)S(1)}, bf16[8,2048]{1,0:T(8,128)(2,1)}, u32[]{:S(2)}) copy-start(bf16[8,2048]{1,0:T(8,128)(2,1)} %param.22) | copy-start | bytes 98308
  0.7 20.6 %copy-start.10 = (bf16[8,2048]{1,0:T(8,128)(2,1)S(1)}, bf16[8,2048]{1,0:T(8,128)(2,1)}, u32[]{:S(2)}) copy-start(bf16[8,2048]{1,0:T(8,128)(2,1)} %param.19) | copy-start | bytes 98308
  4.2 9.6 %collective-permute-start = (bf16[64,256]{1,0:T(8,128)(2,1)S(1)}, bf16[64,256]{1,0:T(8,128)(2,1)S(1)}, u32[]{:S(2)}, u32[]{:S(2)}) collective-permute-start(bf16[64,256]{1,0:T(8,128)(2,1)S(1)} %get-tuple-element.47), channel_id=1, source_target_pairs={{0,8},{8,0},{1,9},{9,1},{2,10},{10,2},{3,11},{11,3},{4,12},{12,4},... | collective-permute-start | bytes 98312 | tf_op jit(solution)/shard_map/ppermute | solution.py:172
  21.2 34.6 %copy-start.8 = (bf16[4,128,128]{2,1,0:T(8,128)(2,1)}, bf16[4,128,128]{2,1,0:T(8,128)(2,1)S(1)}, u32[]{:S(2)}) copy-start(bf16[4,128,128]{2,1,0:T(8,128)(2,1)S(1)} %all_to_all.80.refs_0_) | copy-start | bytes 393220
  21.3 12.5 %collective-permute-start.2 = (bf16[8,8192]{1,0:T(8,128)(2,1)S(1)}, bf16[8,8192]{1,0:T(8,128)(2,1)S(1)}, u32[]{:S(2)}, u32[]{:S(2)}) collective-permute-start(bf16[8,8192]{1,0:T(8,128)(2,1)S(1)} %pad_maximum_fusion.4), channel_id=1, source_target_pairs={{0,4},{1,5},{2,6},{3,7},{4,0},{5,1},{6,2},{7,3},{8,12},{9,13},{10,... | collective-permute-start | bytes 393224 | tf_op jit(solution)/shard_map/ppermute | solution.py:172
  29.5 16.5 %all-to-all-start.1 = ((bf16[8,8,3072]{2,1,0:T(8,128)(2,1)}), bf16[8,8,3072]{2,1,0:T(8,128)(2,1)S(1)}, u32[]{:S(2)}, u32[]{:S(2)}) async-start(bf16[8,8,3072]{2,1,0:T(8,128)(2,1)} %shard_map.165), calls=%async_computation.1 | async-start | bytes 786432 | tf_op jit(solution)/shard_map/all_to_all | solution.py:24
  33.8 21.9 %collective-permute-start.3 = (bf16[16,8192]{1,0:T(8,128)(2,1)S(1)}, bf16[16,8192]{1,0:T(8,128)(2,1)S(1)}, u32[]{:S(2)}, u32[]{:S(2)}) collective-permute-start(bf16[16,8192]{1,0:T(8,128)(2,1)S(1)} %pad_maximum_fusion.2), channel_id=1, source_target_pairs={{0,2},{1,3},{2,0},{3,1},{4,6},{5,7},{6,4},{7,5},{8,10},{9,11},{10,... | collective-permute-start | bytes 786440 | tf_op jit(solution)/shard_map/ppermute | solution.py:172
  46.0 13.1 %copy-start.2 = (bf16[8,8,3072]{2,1,0:T(8,128)(2,1)}, bf16[8,8,3072]{2,1,0:T(8,128)(2,1)S(1)}, u32[]{:S(2)}) copy-start(bf16[8,8,3072]{2,1,0:T(8,128)(2,1)S(1)} %all-to-all-done.1) | copy-start | bytes 1179652
  46.0 13.1 %collective-permute-start.1 = (bf16[64,3072]{1,0:T(8,128)(2,1)S(1)}, bf16[64,3072]{1,0:T(8,128)(2,1)S(1)}, u32[]{:S(2)}, u32[]{:S(2)}) collective-permute-start(bf16[64,3072]{1,0:T(8,128)(2,1)S(1)} %bitcast.18), channel_id=1, source_target_pairs={{0,8},{8,0},{1,9},{9,1},{2,10},{10,2},{3,11},{11,3},{4,12},{12,4},... | collective-permute-start | bytes 1179656 | tf_op jit(solution)/shard_map/ppermute | solution.py:172
  55.8 22.7 %collective-permute-start.4 = (bf16[32,8192]{1,0:T(8,128)(2,1)S(1)}, bf16[32,8192]{1,0:T(8,128)(2,1)S(1)}, u32[]{:S(2)}, u32[]{:S(2)}) collective-permute-start(bf16[32,8192]{1,0:T(8,128)(2,1)S(1)} %pad_maximum_fusion.1), channel_id=1, source_target_pairs={{0,1},{1,0},{2,3},{3,2},{4,5},{5,4},{6,7},{7,6},{8,9},{9,8},{10,11... | collective-permute-start | bytes 1572872 | tf_op jit(solution)/shard_map/ppermute | solution.py:172
  59.1 0.8 copy-start.4
  64.1 8.7 %all-to-all-start.2 = ((bf16[8,64,128]{2,1,0:T(8,128)(2,1)}), bf16[8,64,128]{2,1,0:T(8,128)(2,1)S(1)}, u32[]{:S(2)}, u32[]{:S(2)}) async-start(bf16[8,64,128]{2,1,0:T(8,128)(2,1)} %get-tuple-element.16), calls=%async_computation.2 | async-start | bytes 262144 | tf_op jit(solution)/shard_map/all_to_all | solution.py:24
  72.8 0.7 copy-start.13
  75.1 17.9 %all-to-all-start.3 = ((bf16[8,64,128]{2,1,0:T(8,128)(2,1)}), bf16[8,64,128]{2,1,0:T(8,128)(2,1)S(1)}, u32[]{:S(2)}, u32[]{:S(2)}) async-start(bf16[8,64,128]{2,1,0:T(8,128)(2,1)} %shard_map.168), calls=%async_computation.3 | async-start | bytes 262144 | tf_op jit(solution)/shard_map/all_to_all | solution.py:24
  78.6 14.4 %copy-start.1 = (bf16[64,8192]{1,0:T(8,128)(2,1)}, bf16[64,8192]{1,0:T(8,128)(2,1)S(1)}, u32[]{:S(2)}) copy-start(bf16[64,8192]{1,0:T(8,128)(2,1)S(1)} %pad_maximum_fusion.first_ref.refs_1_.refs_2_) | copy-start | bytes 3145732
  78.6 47.9 %collective-permute-start.5 = (bf16[64,8192]{1,0:T(8,128)(2,1)S(1)}, bf16[64,8192]{1,0:T(8,128)(2,1)S(1)}, u32[]{:S(2)}, u32[]{:S(2)}) collective-permute-start(bf16[64,8192]{1,0:T(8,128)(2,1)S(1)} %pad_maximum_fusion.first_ref.refs_1_.refs_2_), channel_id=1, source_target_pairs={{0,8},{8,0},{1,9},{9,1},{2,10},{10,2},{3,11},{11,3},{4,12},{12,4},... | collective-permute-start | bytes 3145736 | tf_op jit(solution)/shard_map/ppermute | solution.py:172
  93.0 0.6 copy-start.11
  96.8 17.7 %all-to-all-start.4 = ((bf16[16,64,128]{2,1,0:T(8,128)(2,1)}), bf16[16,64,128]{2,1,0:T(8,128)(2,1)S(1)}, u32[]{:S(2)}, u32[]{:S(2)}) async-start(bf16[16,64,128]{2,1,0:T(8,128)(2,1)} %get-tuple-element.18), calls=%async_computation.4 | async-start | bytes 524288 | tf_op jit(solution)/shard_map/all_to_all | solution.py:24
  114.5 0.7 copy-start.7
  116.9 17.6 %all-to-all-start.5 = ((bf16[16,64,128]{2,1,0:T(8,128)(2,1)}), bf16[16,64,128]{2,1,0:T(8,128)(2,1)S(1)}, u32[]{:S(2)}, u32[]{:S(2)}) async-start(bf16[16,64,128]{2,1,0:T(8,128)(2,1)} %shard_map.172), calls=%async_computation.5 | async-start | bytes 524288 | tf_op jit(solution)/shard_map/all_to_all | solution.py:24
  126.5 1.0 copy-start.3
  134.6 0.7 copy-start.6
  140.7 23.2 %all-to-all-start.6 = ((bf16[32,64,128]{2,1,0:T(8,128)(2,1)}), bf16[32,64,128]{2,1,0:T(8,128)(2,1)S(1)}, u32[]{:S(2)}, u32[]{:S(2)}) async-start(bf16[32,64,128]{2,1,0:T(8,128)(2,1)} %get-tuple-element.20), calls=%async_computation.6 | async-start | bytes 1048576 | tf_op jit(solution)/shard_map/all_to_all | solution.py:24
  164.0 0.8 copy-start.5
  254.9 17.4 %copy-start.16 = (bf16[64,128]{1,0:T(8,128)(2,1)S(1)}, bf16[64,128]{1,0:T(8,128)(2,1)}, u32[]{:S(2)}) copy-start(bf16[64,128]{1,0:T(8,128)(2,1)} %get-tuple-element.21) | copy-start | bytes 49156
  254.9 17.5 %copy-start.17 = (bf16[64,128]{1,0:T(8,128)(2,1)S(1)}, bf16[64,128]{1,0:T(8,128)(2,1)}, u32[]{:S(2)}) copy-start(bf16[64,128]{1,0:T(8,128)(2,1)} %get-tuple-element.24) | copy-start | bytes 49156
  268.9 9.1 %all-to-all-start.14 = ((bf16[8,64,128]{2,1,0:T(8,128)(2,1)}), bf16[8,64,128]{2,1,0:T(8,128)(2,1)S(1)}, u32[]{:S(2)}, u32[]{:S(2)}) async-start(bf16[8,64,128]{2,1,0:T(8,128)(2,1)} %get-tuple-element.27), calls=%async_computation.14 | async-start | bytes 262144 | tf_op jit(solution)/shard_map/all_to_all | solution.py:24
  272.5 12.5 %copy-start.15 = (bf16[64,128]{1,0:T(8,128)(2,1)S(1)}, bf16[64,128]{1,0:T(8,128)(2,1)}, u32[]{:S(2)}) copy-start(bf16[64,128]{1,0:T(8,128)(2,1)} %get-tuple-element.26) | copy-start | bytes 49156
  278.0 0.7 copy-start.12
  281.7 8.0 %all-to-all-start.15 = ((bf16[4,64,128]{2,1,0:T(8,128)(2,1)}), bf16[4,64,128]{2,1,0:T(8,128)(2,1)S(1)}, u32[]{:S(2)}, u32[]{:S(2)}) async-start(bf16[4,64,128]{2,1,0:T(8,128)(2,1)} %shard_map.184), calls=%async_computation.15 | async-start | bytes 131072 | tf_op jit(solution)/shard_map/all_to_all | solution.py:24
  292.7 15.6 %collective-permute-start.6 = (bf16[64,256]{1,0:T(8,128)(2,1)S(1)}, bf16[64,256]{1,0:T(8,128)(2,1)S(1)}, u32[]{:S(2)}, u32[]{:S(2)}) collective-permute-start(bf16[64,256]{1,0:T(8,128)(2,1)S(1)} %broadcast_select_fusion.2), channel_id=1, source_target_pairs={{0,8},{8,0},{1,9},{9,1},{2,10},{10,2},{3,11},{11,3},{4,12},{12,4},... | collective-permute-start | bytes 98312 | tf_op jit(solution)/shard_map/ppermute | solution.py:172
  (1 other events, 0.6 us)

commit v3 on v2

--- a/solution.py
+++ b/solution.py
@@ -11,6 +11,7 @@
 BLOCK = 128
 HALF = 64
 CHUNK = 256
+WIDE = 4
 INTERPRET = False
 
 CHIPS = ("ya", "yb", "yc", "x")
@@ -84,6 +85,11 @@
     )
 
 
+def put_blocks(send_ref, at, total):
+    for step in range(WIDE):
+        send_ref[at + step] = total[:, step * BLOCK : (step + 1) * BLOCK].astype(jnp.bfloat16)
+
+
 def forward_kernel(deeper, count, send_count, *refs):
     full_ref, first_ref, second_ref = refs[:3]
     old = refs[3 : 3 + deeper]
@@ -93,12 +99,12 @@
     values = front_values(full_ref, inverse, count).astype(jnp.bfloat16)
     values_ref[...] = values
     stacked = [r[...] for r in old] + [values]
-    for at in range(send_count):
+    for at in range(0, send_count, WIDE):
         total = None
         for left, ref in zip(stacked, couplings):
-            part = dot_nt(left, ref[at * BLOCK : (at + 1) * BLOCK, :])
+            part = dot_nt(left, ref[at * BLOCK : (at + WIDE) * BLOCK, :])
             total = part if total is None else total + part
-        send_ref[at] = total.astype(jnp.bfloat16)
+        put_blocks(send_ref, at, total)
 
 
 def spread_kernel(count, has_own, *refs):
@@ -130,31 +136,57 @@
     for at in range(1, 4):
         total = total + parts_ref[at].astype(jnp.float32)
     values = total.astype(jnp.bfloat16)
-    for at in range(8):
+    for at in range(0, 8, WIDE):
         solved = None
         for part in range(4):
             start = (part * 8 + at) * BLOCK
-            piece = dot_nn(values[:, part * BLOCK : (part + 1) * BLOCK], inverse[:, start : start + BLOCK])
+            piece = dot_nn(values[:, part * BLOCK : (part + 1) * BLOCK], inverse[:, start : start + WIDE * BLOCK])
             solved = piece if solved is None else solved + piece
-        send_ref[at] = solved.astype(jnp.bfloat16)
-
-
-def backward_kernel(depth, *refs):
-    solved = refs[:depth]
-    values_ref, first_ref, second_ref = refs[depth : depth + 3]
-    couplings = refs[depth + 3 : 2 * depth + 3]
+        put_blocks(send_ref, at, solved)
+
+
+def pulled(total, solved, couplings, first):
+    for upper, (full_ref, coupling_ref) in enumerate(zip(solved, couplings), first):
+
+        def product(left, at):
+            return dot_nn(left, coupling_ref[at * BLOCK : (at + 2) * BLOCK, :])
+
+        total = total - pairs_product(full_ref, product, GROUP_SIZE[upper])
+    return total
+
+
+def top_pull_kernel(full_ref, *refs):
+    count = len(refs) // 3
+    for at in range(count):
+        total = refs[at][...].astype(jnp.float32)
+        refs[2 * count + at][...] = pulled(total, [full_ref], [refs[count + at]], 0)
+
+
+def backward_kernel(depth, first, *refs):
+    count = depth - first
+    values_ref, first_ref, second_ref = refs[count : count + 3]
     send_ref = refs[-1]
     total = values_ref[...].astype(jnp.float32)
-    for upper in range(depth):
-
-        def product(left, at):
-            return dot_nn(left, couplings[upper][at * BLOCK : (at + 2) * BLOCK, :])
-
-        total = total - pairs_product(solved[upper], product, GROUP_SIZE[upper])
-    adjusted = total.astype(jnp.bfloat16)
+    adjusted = pulled(total, refs[:count], refs[count + 3 : -1], first).astype(jnp.bfloat16)
     inverse = jnp.concatenate([first_ref[...], second_ref[...]], axis=0)
-    for at in range(GROUP_SIZE[depth]):
-        send_ref[at] = dot_nn(adjusted, inverse[:, at * BLOCK : (at + 1) * BLOCK]).astype(jnp.bfloat16)
+    if depth == LEVELS - 1:
+        solved = dot_nn(adjusted, inverse)
+        for at in range(2 * GROUP_SIZE[depth]):
+            block = solved[:, at * HALF : (at + 1) * HALF]
+            send_ref[at] = jnp.concatenate([block[: HALF // 2], block[HALF // 2 :]], axis=1).astype(jnp.bfloat16)
+        return
+    for at in range(0, GROUP_SIZE[depth], WIDE):
+        put_blocks(send_ref, at, dot_nn(adjusted, inverse[:, at * BLOCK : (at + WIDE) * BLOCK]))
+
+
+def final_kernel(parts_ref, out_ref):
+    halves = []
+    for core in range(2):
+        total = parts_ref[core].astype(jnp.float32)
+        for at in range(1, GROUP_SIZE[-1]):
+            total = total + parts_ref[2 * at + core].astype(jnp.float32)
+        halves += [total[:, :HALF], total[:, HALF:]]
+    out_ref[...] = jnp.concatenate(halves, axis=0).T.astype(jnp.bfloat16)
 
 
 def copies_kernel(*refs):
@@ -170,6 +202,16 @@
 def partner(value, axis, mask):
     size = lax.axis_size(axis)
     return lax.ppermute(value, axis, [(at, at ^ mask) for at in range(size)])
+
+
+def by_chip(blocks):
+    chip = lax.axis_index("x")
+    odd = (chip & 1) == 1
+    high = (chip & 2) == 2
+    pairs = []
+    for at in (0, 2):
+        pairs += [jnp.where(odd, blocks[at + 1], blocks[at]), jnp.where(odd, blocks[at], blocks[at + 1])]
+    return [jnp.where(high, pairs[at ^ 2], pairs[at]) for at in range(4)]
 
 
 def in_order(mine, other, axis):
@@ -192,10 +234,12 @@
     other = partner(lax.dynamic_slice_in_dim(stacked, (1 - core) * HALF, HALF, 0), "c", 1)
     rhs = [in_order(mine[:, k * HALF : (k + 1) * HALF], other[:, k * HALF : (k + 1) * HALF], 1) for k in range(LEVELS)]
     low = [low, partner(low, "c", 1)]
-    top = inv_0.reshape(shard_rows, 8, 4, BLOCK).transpose(2, 1, 0, 3).reshape(4, 8 * shard_rows, BLOCK)
-    sent = jnp.concatenate([jnp.broadcast_to(rhs[3][None], (4, HALF, BLOCK)), top], axis=1)
-    full = exchange(sent, "x")
-    top = full[:, HALF:].reshape(32, shard_rows, BLOCK).transpose(1, 0, 2).reshape(shard_rows, 4096)
+    full = jnp.stack(by_chip([rhs[3]] + [partner(rhs[3], "x", mask) for mask in (1, 2, 3)]))
+    top = inv_0.reshape(shard_rows, 8, 4, BLOCK).transpose(2, 0, 1, 3).reshape(4, shard_rows, 8 * BLOCK)
+    spot = lax.axis_index("x")
+    tops = [lax.dynamic_index_in_dim(top, spot ^ mask, 0, keepdims=False) for mask in range(4)]
+    top = by_chip(tops[:1] + [partner(tops[mask], "x", mask) for mask in (1, 2, 3)])
+    top = jnp.concatenate(top, axis=1)
     high = jnp.concatenate([inv_1, coupling_1, top], axis=1)
     mask = panels // 2
     while mask:
@@ -223,7 +267,6 @@
     exp = [None, [near_1], [to_0(far_2), near_2], [to_0(far_3), far_31, near_3]]
 
     values = [None] * LEVELS
-    full = (full, (4, HALF, BLOCK), (0, 0, 0))
     for k in (3, 2, 1):
         send_count = GROUP_SIZE[k - 1]
         order = list(range(3, k, -1))
@@ -243,26 +286,38 @@
     parts = call(root_solve_kernel, [bf16(8, HALF, BLOCK)], [parts] + inv[0])[0]
     solved = []
     out = []
-    for k in range(LEVELS):
+    for k in range(LEVELS - 1):
         parts = exchange(parts, GROUP_AXES[k] if k else COLUMN)
         kernel = functools.partial(spread_kernel, GROUP_SIZE[k] if k else 8, 0)
-        if k == LEVELS - 1:
-            out.append(call(kernel, [bf16(HALF, BLOCK)], [parts])[0])
-            break
         sent, own = call(kernel, [bf16(GROUP_SIZE[k], HALF, BLOCK), bf16(HALF, BLOCK)], [parts])
         out.append(own)
         solved.append(exchange(sent, GROUP_AXES[k]))
+        if k == 1:
+            values[2:] = call(
+                top_pull_kernel,
+                [jax.ShapeDtypeStruct((HALF, BLOCK), jnp.float32)] * 2,
+                [solved[0]] + values[2:] + [exp[2][0], exp[3][0]],
+            )
+        first = 1 if k else 0
+        send_shape = bf16(GROUP_SIZE[k + 1], HALF, BLOCK) if k < LEVELS - 2 else bf16(8, HALF // 2, BLOCK)
         parts = call(
-            functools.partial(backward_kernel, k + 1),
-            [bf16(GROUP_SIZE[k + 1], HALF, BLOCK)],
-            solved + [values[k + 1]] + inv[k + 1] + exp[k + 1],
+            functools.partial(backward_kernel, k + 1, first),
+            [send_shape],
+            solved[first:] + [values[k + 1]] + inv[k + 1] + exp[k + 1][first:],
         )[0]
-    lows = jnp.concatenate([o[:, :HALF] for o in out], axis=1)
-    highs = jnp.concatenate([o[:, HALF:] for o in out], axis=1)
+    outputs = returned(out[:2], core) + returned(out[2:], core)
+    parts = exchange(parts, ("x", "c"))
+    outputs += call(final_kernel, [bf16(HALF, BLOCK)], [parts])
+    return tuple(outputs)
+
+
+def returned(solved, core):
+    lows = jnp.concatenate([o[:, :HALF] for o in solved], axis=1)
+    highs = jnp.concatenate([o[:, HALF:] for o in solved], axis=1)
     low_core = core == 0
     other = partner(jnp.where(low_core, highs, lows), "c", 1)
     rows = in_order(jnp.where(low_core, lows, highs), other, 0).T
-    return tuple(rows[k * HALF : (k + 1) * HALF] for k in range(LEVELS))
+    return [rows[k * HALF : (k + 1) * HALF] for k in range(len(solved))]
 
 
 def solution(mesh):

time: 314 us -> 308 us (0.981)
  blocking collectives: 93.9 us -> 64.2 us
  starting transfers between devices: 85.6 us -> 112 us
  waiting for transfers between devices: 50.5 us -> 42.2 us
    all_to_all x8 -> x5, blocking collectives: 93.9 us -> 64.2 us  [exchange(): return lax.all_to_all(value, axes, 0, 0, tiled=True)]
    ppermute x7 -> x14, starting transfers between devices: 48.6 us -> 64.3 us  [partner(): return lax.ppermute(value, axis, [(at, at ^ mask) for at in range(size)])]
    all_to_all x8 -> x10, starting transfers between devices: 37.1 us -> 48.2 us  [exchange(): return lax.all_to_all(value, axes, 0, 0, tiled=True)]
    all_to_all x8 -> x10, waiting for transfers between devices: 46.8 us -> 38.5 us  [exchange(): return lax.all_to_all(value, axes, 0, 0, tiled=True)]
    unnamed x44 -> x39, local copies, waits for them, and re-layouts: 12.7 us -> 14.9 us
    pallas_call x21 -> x22, Pallas kernels: 59.6 us -> 59.7 us  [call(): pl.pallas_call(kernel, grid=(1,), in_specs=specs, out_specs=out_specs, ou...]
  transfers between devices with their start and end apart: 15 -> 24, of which waited for: 8 -> 6; matrix products, arithmetic and copies ran while one was open for 2% -> 5% of each run, Pallas kernels for 10% -> 12%
where the time goes in v3:
time: 308 us; the launch traced here: 305 us
  starting transfers between devices  112 us (36%)
  blocking collectives  64.2 us (21%)
  Pallas kernels  59.7 us (19%)
  waiting for transfers between devices  42.2 us (14%)
  local copies, waits for them, and re-layouts  20 us (6%)
  other arithmetic  5.1 us (2%)
    ppermute x14, starting transfers between devices, partner(): return lax.ppermute(value, axis, [(at, at ^ mask) for at in range(size)])  64.3 us
    all_to_all x5, blocking collectives, exchange(): return lax.all_to_all(value, axes, 0, 0, tiled=True)  64.2 us
    pallas_call x22, Pallas kernels, call(): pl.pallas_call(kernel, grid=(1,), in_specs=specs, out_specs=out_specs, ou...  59.7 us
    all_to_all x10, starting transfers between devices, exchange(): return lax.all_to_all(value, axes, 0, 0, tiled=True)  48.2 us
    all_to_all x10, waiting for transfers between devices, exchange(): return lax.all_to_all(value, axes, 0, 0, tiled=True)  38.5 us
    unnamed x39, local copies, waits for them, and re-layouts  14.9 us
  transfers between devices with their start and end apart: 24, of which 6 were waited for; matrix products, arithmetic and copies ran while one was open for 5% of the time, Pallas kernels for 12%

profile of v3, /device:TPU:1, one launch (start us, length us, event | category | flops | bytes accessed | tf_op | source)
XLA Modules:
  0.0 304.8 jit_solution(12737262737086095366)
XLA Ops:
  1.6 3.9 %collective-permute-start.7 = (bf16[8,1024]{1,0:T(8,128)(2,1)S(1)}, bf16[8,1024]{1,0:T(8,128)(2,1)S(1)}, u32[]{:S(2)}, u32[]{:S(2)}) collective-permute-start(bf16[8,1024]{1,0:T(8,128)(2,1)S(1)} %get-tuple-element.46), channel_id=1, source_target_pairs={{0,16},{16,0},{32,48},{48,32},{1,17},{17,1},{33,49},{49,33},{2,18}... | collective-permute-start | bytes 49160 | tf_op jit(solution)/shard_map/ppermute | solution.py:204
  5.5 4.4 %collective-permute-start.6 = (bf16[8,1024]{1,0:T(8,128)(2,1)S(1)}, bf16[8,1024]{1,0:T(8,128)(2,1)S(1)}, u32[]{:S(2)}, u32[]{:S(2)}) collective-permute-start(bf16[8,1024]{1,0:T(8,128)(2,1)S(1)} %get-tuple-element.47), channel_id=1, source_target_pairs={{0,32},{16,48},{32,0},{48,16},{1,33},{17,49},{33,1},{49,17},{2,34}... | collective-permute-start | bytes 49160 | tf_op jit(solution)/shard_map/ppermute | solution.py:204
  16.9 10.8 %collective-permute-start.8 = (bf16[8,8192]{1,0:T(8,128)(2,1)S(1)}, bf16[8,8192]{1,0:T(8,128)(2,1)S(1)}, u32[]{:S(2)}, u32[]{:S(2)}) collective-permute-start(bf16[8,8192]{1,0:T(8,128)(2,1)S(1)} %select_dynamic-update-slice_fusion), channel_id=1, source_target_pairs={{0,4},{1,5},{2,6},{3,7},{4,0},{5,1},{6,2},{7,3},{8,12},{9,13},{10,... | collective-permute-start | bytes 393224 | tf_op jit(solution)/shard_map/ppermute | solution.py:204
  27.8 3.7 %collective-permute-start = (bf16[64,256]{1,0:T(8,128)(2,1)S(1)}, bf16[64,256]{1,0:T(8,128)(2,1)S(1)}, u32[]{:S(2)}, u32[]{:S(2)}) collective-permute-start(bf16[64,256]{1,0:T(8,128)(2,1)S(1)} %get-tuple-element.54), channel_id=1, source_target_pairs={{0,8},{8,0},{1,9},{9,1},{2,10},{10,2},{3,11},{11,3},{4,12},{12,4},... | collective-permute-start | bytes 98312 | tf_op jit(solution)/shard_map/ppermute | solution.py:204
  33.0 4.3 %all-to-all-start = ((bf16[8,8,3072]{2,1,0:T(8,128)(2,1)}), bf16[8,8,3072]{2,1,0:T(8,128)(2,1)S(1)}, u32[]{:S(2)}, u32[]{:S(2)}) async-start(bf16[8,8,3072]{2,1,0:T(8,128)(2,1)} %shard_map.165), calls=%async_computation | async-start | bytes 786432 | tf_op jit(solution)/shard_map/all_to_all | solution.py:25
  38.6 4.3 %collective-permute-start.9 = (bf16[16,8192]{1,0:T(8,128)(2,1)S(1)}, bf16[16,8192]{1,0:T(8,128)(2,1)S(1)}, u32[]{:S(2)}, u32[]{:S(2)}) collective-permute-start(bf16[16,8192]{1,0:T(8,128)(2,1)S(1)} %pad_maximum_fusion.2), channel_id=1, source_target_pairs={{0,2},{1,3},{2,0},{3,1},{4,6},{5,7},{6,4},{7,5},{8,10},{9,11},{10,... | collective-permute-start | bytes 786440 | tf_op jit(solution)/shard_map/ppermute | solution.py:204
  45.0 5.6 %collective-permute-start.2 = (bf16[64,128]{1,0:T(8,128)(2,1)S(1)}, bf16[64,128]{1,0:T(8,128)(2,1)S(1)}, u32[]{:S(2)}, u32[]{:S(2)}) collective-permute-start(bf16[64,128]{1,0:T(8,128)(2,1)S(1)} %pad_maximum_fusion.5), channel_id=1, source_target_pairs={{0,32},{16,48},{32,0},{48,16},{1,33},{17,49},{33,1},{49,17},{2,34}... | collective-permute-start | bytes 49160 | tf_op jit(solution)/shard_map/ppermute | solution.py:204
  52.7 3.6 %collective-permute-start.4 = (bf16[64,3072]{1,0:T(8,128)(2,1)S(1)}, bf16[64,3072]{1,0:T(8,128)(2,1)S(1)}, u32[]{:S(2)}, u32[]{:S(2)}) collective-permute-start(bf16[64,3072]{1,0:T(8,128)(2,1)S(1)} %bitcast.40), channel_id=1, source_target_pairs={{0,8},{8,0},{1,9},{9,1},{2,10},{10,2},{3,11},{11,3},{4,12},{12,4},... | collective-permute-start | bytes 1179656 | tf_op jit(solution)/shard_map/ppermute | solution.py:204
  56.3 3.7 %collective-permute-done.9 = bf16[16,8192]{1,0:T(8,128)(2,1)S(1)} collective-permute-done((bf16[16,8192]{1,0:T(8,128)(2,1)S(1)}, bf16[16,8192]{1,0:T(8,128)(2,1)S(1)}, u32[]{:S(2)}, u32[]{:S(2)}) %collective-permute-start.9) | collective-permute-done | bytes 262176 | tf_op jit(solution)/shard_map/ppermute | solution.py:204
  67.6 4.8 %all-to-all-start.1 = ((bf16[8,64,128]{2,1,0:T(8,128)(2,1)}), bf16[8,64,128]{2,1,0:T(8,128)(2,1)S(1)}, u32[]{:S(2)}, u32[]{:S(2)}) async-start(bf16[8,64,128]{2,1,0:T(8,128)(2,1)} %get-tuple-element.18), calls=%async_computation.1 | async-start | bytes 262144 | tf_op jit(solution)/shard_map/all_to_all | solution.py:25
  73.1 4.7 %all-to-all-done.1.refs_0_ = bf16[8,64,128]{2,1,0:T(8,128)(2,1)S(1)} async-done(((bf16[8,64,128]{2,1,0:T(8,128)(2,1)}), bf16[8,64,128]{2,1,0:T(8,128)(2,1)S(1)}, u32[]{:S(2)}, u32[]{:S(2)}) %all-to-all-start.1) | async-done | bytes 131104 | tf_op jit(solution)/shard_map/all_to_all | solution.py:25
  83.5 4.5 %collective-permute-start.11 = (bf16[64,8192]{1,0:T(8,128)(2,1)S(1)}, bf16[64,8192]{1,0:T(8,128)(2,1)S(1)}, u32[]{:S(2)}, u32[]{:S(2)}) collective-permute-start(bf16[64,8192]{1,0:T(8,128)(2,1)S(1)} %pad_maximum_fusion.first_ref.refs_1_.refs_2_), channel_id=1, source_target_pairs={{0,8},{8,0},{1,9},{9,1},{2,10},{10,2},{3,11},{11,3},{4,12},{12,4},... | collective-permute-start | bytes 3145736 | tf_op jit(solution)/shard_map/ppermute | solution.py:204
  89.4 4.8 %shard_map.169.refs_4_.refs_5_.refs_3_ = bf16[6144,128]{1,0:T(8,128)(2,1)} custom-call(s32[1,512]{1,0:T(1,128)} %constant_dynamic-slice_fusion.2.list_ref, bf16[64,3072]{1,0:T(8,128)(2,1)} %bitcast.43, bf16[64,3072]{1,0:T(8,128)(2,1)} %copy-done.4), custom_call_target="tpu_custom_call" | custom-call | tf_op jit(solution)/shard_map/pallas_call | solution.py:44
  100.9 7.5 %all-to-all-start.3 = ((bf16[16,64,128]{2,1,0:T(8,128)(2,1)}), bf16[16,64,128]{2,1,0:T(8,128)(2,1)S(1)}, u32[]{:S(2)}, u32[]{:S(2)}) async-start(bf16[16,64,128]{2,1,0:T(8,128)(2,1)} %get-tuple-element.20), calls=%async_computation.3 | async-start | bytes 524288 | tf_op jit(solution)/shard_map/all_to_all | solution.py:25
  109.1 9.5 %all-to-all-done.3.refs_0_ = bf16[16,64,128]{2,1,0:T(8,128)(2,1)S(1)} async-done(((bf16[16,64,128]{2,1,0:T(8,128)(2,1)}), bf16[16,64,128]{2,1,0:T(8,128)(2,1)S(1)}, u32[]{:S(2)}, u32[]{:S(2)}) %all-to-all-start.3) | async-done | bytes 262176 | tf_op jit(solution)/shard_map/all_to_all | solution.py:25
  121.0 4.1 %all-to-all-start.4 = ((bf16[16,64,128]{2,1,0:T(8,128)(2,1)}), bf16[16,64,128]{2,1,0:T(8,128)(2,1)S(1)}, u32[]{:S(2)}, u32[]{:S(2)}) async-start(bf16[16,64,128]{2,1,0:T(8,128)(2,1)} %shard_map.172), calls=%async_computation.4 | async-start | bytes 524288 | tf_op jit(solution)/shard_map/all_to_all | solution.py:25
  125.7 4.8 %shard_map.173.refs_6_.refs_2_ = bf16[4096,128]{1,0:T(8,128)(2,1)} custom-call(s32[1,1024]{1,0:T(1,128)} %constant_dynamic-slice_fusion.1.list_ref, bf16[64,3072]{1,0:T(8,128)(2,1)} %bitcast.46, bf16[64,3072]{1,0:T(8,128)(2,1)} %copy-done.4), custom_call_target="tpu_custom_call" | custom-call | tf_op jit(solution)/shard_map/pallas_call | solution.py:44
  131.5 7.1 %shard_map.174.refs_7_.refs_4_ = bf16[4096,128]{1,0:T(8,128)(2,1)} custom-call(s32[1,2048]{1,0:T(1,128)} %constant_dynamic-slice_fusion.list_ref, bf16[64,8192]{1,0:T(8,128)(2,1)} %copy-done.1, bf16[64,8192]{1,0:T(8,128)(2,1)} %copy-done.3), custom_call_target="tpu_custom_call" | custom-call | tf_op jit(solution)/shard_map/pallas_call | solution.py:44
  139.3 4.3 %shard_map.175 = (bf16[64,128]{1,0:T(8,128)(2,1)}, bf16[32,64,128]{2,1,0:T(8,128)(2,1)}) custom-call(bf16[16,64,128]{2,1,0:T(8,128)(2,1)} %copy-done.7, bf16[64,8192]{1,0:T(8,128)(2,1)} %copy-done.1, bf16[64,8192]{1,0:T(8,128)(2,1)} %copy-done.3, bf16[64,128]{1,0:T(8,128)(2,1)} %get-tuple-element.19.refs_3_.refs_1_, ...), custom_call_target="tpu_custom_call" | custom-call | tf_op jit(solution)/shard_map/pallas_call | solution.py:44
  143.7 7.2 %all-to-all-start.5 = ((bf16[32,64,128]{2,1,0:T(8,128)(2,1)}), bf16[32,64,128]{2,1,0:T(8,128)(2,1)S(1)}, u32[]{:S(2)}, u32[]{:S(2)}) async-start(bf16[32,64,128]{2,1,0:T(8,128)(2,1)} %get-tuple-element.22), calls=%async_computation.5 | async-start | bytes 1048576 | tf_op jit(solution)/shard_map/all_to_all | solution.py:25
  151.6 14.7 %all-to-all-done.5.refs_0_ = bf16[32,64,128]{2,1,0:T(8,128)(2,1)S(1)} async-done(((bf16[32,64,128]{2,1,0:T(8,128)(2,1)}), bf16[32,64,128]{2,1,0:T(8,128)(2,1)S(1)}, u32[]{:S(2)}, u32[]{:S(2)}) %all-to-all-start.5) | async-done | bytes 524320 | tf_op jit(solution)/shard_map/all_to_all | solution.py:25
  168.9 12.0 %all_to_all.75.full_ref = bf16[8,64,128]{2,1,0:T(8,128)(2,1)} all-to-all(bf16[8,64,128]{2,1,0:T(8,128)(2,1)} %shard_map.176), channel_id=1, replica_groups=mesh['ya'=2,'yb'=2,'yc'=2,'x'=4,'c'=2,'z'=8] {'ya','yb','yc'}, dimensions={0} | all-to-all | bytes 262144 | tf_op jit(solution)/shard_map/all_to_all | solution.py:25
  183.3 9.8 %all_to_all.76.parts_ref = bf16[4,64,512]{2,1,0:T(8,128)(2,1)} all-to-all(bf16[4,64,512]{2,1,0:T(8,128)(2,1)} %shard_map.177), channel_id=1, replica_groups=mesh['ya'=2,'yb'=2,'yc'=2,'x'=4,'c'=2,'z'=8] {'x'}, dimensions={0} | all-to-all | bytes 524288 | tf_op jit(solution)/shard_map/all_to_all | solution.py:25
  195.3 11.9 %all_to_all.77.refs_0_ = bf16[8,64,128]{2,1,0:T(8,128)(2,1)} all-to-all(bf16[8,64,128]{2,1,0:T(8,128)(2,1)} %shard_map.178), channel_id=1, replica_groups=mesh['ya'=2,'yb'=2,'yc'=2,'x'=4,'c'=2,'z'=8] {'ya','yb','yc'}, dimensions={0} | all-to-all | bytes 262144 | tf_op jit(solution)/shard_map/all_to_all | solution.py:25
  209.0 17.5 %all_to_all.78.refs_0_.full_ref = bf16[32,64,128]{2,1,0:T(8,128)(2,1)} all-to-all(bf16[32,64,128]{2,1,0:T(8,128)(2,1)} %get-tuple-element.24), channel_id=1, replica_groups=mesh['ya'=2,'yb'=2,'yc'=2,'x'=4,'c'=2,'z'=8] {'ya','yb','yc','x'}, dimensions={0} | all-to-all | bytes 1048576 | tf_op jit(solution)/shard_map/all_to_all | solution.py:25
  229.3 13.0 %all_to_all.79.refs_0_ = bf16[16,64,128]{2,1,0:T(8,128)(2,1)} all-to-all(bf16[16,64,128]{2,1,0:T(8,128)(2,1)} %shard_map.180), channel_id=1, replica_groups=mesh['ya'=2,'yb'=2,'yc'=2,'x'=4,'c'=2,'z'=8] {'yb','yc','x'}, dimensions={0} | all-to-all | bytes 524288 | tf_op jit(solution)/shard_map/all_to_all | solution.py:25
  248.7 10.5 %collective-permute-start.12 = (bf16[64,128]{1,0:T(8,128)(2,1)S(1)}, bf16[64,128]{1,0:T(8,128)(2,1)S(1)}, u32[]{:S(2)}, u32[]{:S(2)}) collective-permute-start(bf16[64,128]{1,0:T(8,128)(2,1)S(1)} %broadcast_select_fusion.20), channel_id=1, source_target_pairs={{0,8},{8,0},{1,9},{9,1},{2,10},{10,2},{3,11},{11,3},{4,12},{12,4},... | collective-permute-start | bytes 49160 | tf_op jit(solution)/shard_map/ppermute | solution.py:204
  265.1 5.2 %all-to-all-start.12 = ((bf16[8,64,128]{2,1,0:T(8,128)(2,1)}), bf16[8,64,128]{2,1,0:T(8,128)(2,1)S(1)}, u32[]{:S(2)}, u32[]{:S(2)}) async-start(bf16[8,64,128]{2,1,0:T(8,128)(2,1)} %shard_map.183), calls=%async_computation.12 | async-start | bytes 262144 | tf_op jit(solution)/shard_map/all_to_all | solution.py:25
  270.4 5.3 %all-to-all-done.12.refs_0_ = bf16[8,64,128]{2,1,0:T(8,128)(2,1)S(1)} async-done(((bf16[8,64,128]{2,1,0:T(8,128)(2,1)}), bf16[8,64,128]{2,1,0:T(8,128)(2,1)S(1)}, u32[]{:S(2)}, u32[]{:S(2)}) %all-to-all-start.12) | async-done | bytes 131104 | tf_op jit(solution)/shard_map/all_to_all | solution.py:25
  282.3 5.2 %collective-permute-start.13 = (bf16[64,64]{1,0:T(8,128)(2,1)S(1)}, bf16[64,64]{1,0:T(8,128)(2,1)S(1)}, u32[]{:S(2)}, u32[]{:S(2)}) collective-permute-start(bf16[64,64]{1,0:T(8,128)(2,1)S(1)} %broadcast_select_fusion.4), channel_id=1, source_target_pairs={{0,8},{8,0},{1,9},{9,1},{2,10},{10,2},{3,11},{11,3},{4,12},{12,4},... | collective-permute-start | bytes 24584 | tf_op jit(solution)/shard_map/ppermute | solution.py:204
  292.9 4.8 %all-to-all-start.14 = ((bf16[8,32,128]{2,1,0:T(8,128)(2,1)}), bf16[8,32,128]{2,1,0:T(8,128)(2,1)S(1)}, u32[]{:S(2)}, u32[]{:S(2)}) async-start(bf16[8,32,128]{2,1,0:T(8,128)(2,1)} %shard_map.185), calls=%async_computation.14 | async-start | bytes 131072 | tf_op jit(solution)/shard_map/all_to_all | solution.py:25
  298.4 4.1 %all-to-all-done.14.parts_ref = bf16[8,32,128]{2,1,0:T(8,128)(2,1)S(1)} async-done(((bf16[8,32,128]{2,1,0:T(8,128)(2,1)}), bf16[8,32,128]{2,1,0:T(8,128)(2,1)S(1)}, u32[]{:S(2)}, u32[]{:S(2)}) %all-to-all-start.14) | async-done | bytes 65568 | tf_op jit(solution)/shard_map/all_to_all | solution.py:25
  (112 shorter events, 82.0 us)
Async XLA Ops:
  0.6 124.5 %copy-start = (s32[2,2048]{1,0:T(2,128)S(1)}, s32[2,2048]{1,0:T(2,128)}, u32[]{:S(2)}) copy-start(s32[2,2048]{1,0:T(2,128)} %param.25) | copy-start | bytes 49156
  1.6 15.2 %collective-permute-start.7 = (bf16[8,1024]{1,0:T(8,128)(2,1)S(1)}, bf16[8,1024]{1,0:T(8,128)(2,1)S(1)}, u32[]{:S(2)}, u32[]{:S(2)}) collective-permute-start(bf16[8,1024]{1,0:T(8,128)(2,1)S(1)} %get-tuple-element.46), channel_id=1, source_target_pairs={{0,16},{16,0},{32,48},{48,32},{1,17},{17,1},{33,49},{49,33},{2,18}... | collective-permute-start | bytes 49160 | tf_op jit(solution)/shard_map/ppermute | solution.py:204
  5.5 11.3 %collective-permute-start.6 = (bf16[8,1024]{1,0:T(8,128)(2,1)S(1)}, bf16[8,1024]{1,0:T(8,128)(2,1)S(1)}, u32[]{:S(2)}, u32[]{:S(2)}) collective-permute-start(bf16[8,1024]{1,0:T(8,128)(2,1)S(1)} %get-tuple-element.47), channel_id=1, source_target_pairs={{0,32},{16,48},{32,0},{48,16},{1,33},{17,49},{33,1},{49,17},{2,34}... | collective-permute-start | bytes 49160 | tf_op jit(solution)/shard_map/ppermute | solution.py:204
  9.9 6.9 %collective-permute-start.5 = (bf16[8,1024]{1,0:T(8,128)(2,1)S(1)}, bf16[8,1024]{1,0:T(8,128)(2,1)S(1)}, u32[]{:S(2)}, u32[]{:S(2)}) collective-permute-start(bf16[8,1024]{1,0:T(8,128)(2,1)S(1)} %get-tuple-element.48), channel_id=1, source_target_pairs={{0,48},{16,32},{32,16},{48,0},{1,49},{17,33},{33,17},{49,1},{2,50}... | collective-permute-start | bytes 49160 | tf_op jit(solution)/shard_map/ppermute | solution.py:204
  16.9 21.7 %collective-permute-start.8 = (bf16[8,8192]{1,0:T(8,128)(2,1)S(1)}, bf16[8,8192]{1,0:T(8,128)(2,1)S(1)}, u32[]{:S(2)}, u32[]{:S(2)}) collective-permute-start(bf16[8,8192]{1,0:T(8,128)(2,1)S(1)} %select_dynamic-update-slice_fusion), channel_id=1, source_target_pairs={{0,4},{1,5},{2,6},{3,7},{4,0},{5,1},{6,2},{7,3},{8,12},{9,13},{10,... | collective-permute-start | bytes 393224 | tf_op jit(solution)/shard_map/ppermute | solution.py:204
  27.8 15.1 %collective-permute-start = (bf16[64,256]{1,0:T(8,128)(2,1)S(1)}, bf16[64,256]{1,0:T(8,128)(2,1)S(1)}, u32[]{:S(2)}, u32[]{:S(2)}) collective-permute-start(bf16[64,256]{1,0:T(8,128)(2,1)S(1)} %get-tuple-element.54), channel_id=1, source_target_pairs={{0,8},{8,0},{1,9},{9,1},{2,10},{10,2},{3,11},{11,3},{4,12},{12,4},... | collective-permute-start | bytes 98312 | tf_op jit(solution)/shard_map/ppermute | solution.py:204
  33.0 19.7 %all-to-all-start = ((bf16[8,8,3072]{2,1,0:T(8,128)(2,1)}), bf16[8,8,3072]{2,1,0:T(8,128)(2,1)S(1)}, u32[]{:S(2)}, u32[]{:S(2)}) async-start(bf16[8,8,3072]{2,1,0:T(8,128)(2,1)} %shard_map.165), calls=%async_computation | async-start | bytes 786432 | tf_op jit(solution)/shard_map/all_to_all | solution.py:25
  38.6 21.4 %collective-permute-start.9 = (bf16[16,8192]{1,0:T(8,128)(2,1)S(1)}, bf16[16,8192]{1,0:T(8,128)(2,1)S(1)}, u32[]{:S(2)}, u32[]{:S(2)}) collective-permute-start(bf16[16,8192]{1,0:T(8,128)(2,1)S(1)} %pad_maximum_fusion.2), channel_id=1, source_target_pairs={{0,2},{1,3},{2,0},{3,1},{4,6},{5,7},{6,4},{7,5},{8,10},{9,11},{10,... | collective-permute-start | bytes 786440 | tf_op jit(solution)/shard_map/ppermute | solution.py:204
  43.1 18.9 %collective-permute-start.3 = (bf16[64,128]{1,0:T(8,128)(2,1)S(1)}, bf16[64,128]{1,0:T(8,128)(2,1)S(1)}, u32[]{:S(2)}, u32[]{:S(2)}) collective-permute-start(bf16[64,128]{1,0:T(8,128)(2,1)S(1)} %pad_maximum_fusion.5), channel_id=1, source_target_pairs={{0,16},{16,0},{32,48},{48,32},{1,17},{17,1},{33,49},{49,33},{2,18}... | collective-permute-start | bytes 49160 | tf_op jit(solution)/shard_map/ppermute | solution.py:204
  45.0 17.0 %collective-permute-start.2 = (bf16[64,128]{1,0:T(8,128)(2,1)S(1)}, bf16[64,128]{1,0:T(8,128)(2,1)S(1)}, u32[]{:S(2)}, u32[]{:S(2)}) collective-permute-start(bf16[64,128]{1,0:T(8,128)(2,1)S(1)} %pad_maximum_fusion.5), channel_id=1, source_target_pairs={{0,32},{16,48},{32,0},{48,16},{1,33},{17,49},{33,1},{49,17},{2,34}... | collective-permute-start | bytes 49160 | tf_op jit(solution)/shard_map/ppermute | solution.py:204
  50.6 11.4 %collective-permute-start.1 = (bf16[64,128]{1,0:T(8,128)(2,1)S(1)}, bf16[64,128]{1,0:T(8,128)(2,1)S(1)}, u32[]{:S(2)}, u32[]{:S(2)}) collective-permute-start(bf16[64,128]{1,0:T(8,128)(2,1)S(1)} %pad_maximum_fusion.5), channel_id=1, source_target_pairs={{0,48},{16,32},{32,16},{48,0},{1,49},{17,33},{33,17},{49,1},{2,50}... | collective-permute-start | bytes 49160 | tf_op jit(solution)/shard_map/ppermute | solution.py:204
  52.7 10.0 %copy-start.2 = (bf16[8,8,3072]{2,1,0:T(8,128)(2,1)}, bf16[8,8,3072]{2,1,0:T(8,128)(2,1)S(1)}, u32[]{:S(2)}) copy-start(bf16[8,8,3072]{2,1,0:T(8,128)(2,1)S(1)} %all-to-all-done) | copy-start | bytes 1179652
  52.7 10.0 %collective-permute-start.4 = (bf16[64,3072]{1,0:T(8,128)(2,1)S(1)}, bf16[64,3072]{1,0:T(8,128)(2,1)S(1)}, u32[]{:S(2)}, u32[]{:S(2)}) collective-permute-start(bf16[64,3072]{1,0:T(8,128)(2,1)S(1)} %bitcast.40), channel_id=1, source_target_pairs={{0,8},{8,0},{1,9},{9,1},{2,10},{10,2},{3,11},{11,3},{4,12},{12,4},... | collective-permute-start | bytes 1179656 | tf_op jit(solution)/shard_map/ppermute | solution.py:204
  60.1 23.4 %collective-permute-start.10 = (bf16[32,8192]{1,0:T(8,128)(2,1)S(1)}, bf16[32,8192]{1,0:T(8,128)(2,1)S(1)}, u32[]{:S(2)}, u32[]{:S(2)}) collective-permute-start(bf16[32,8192]{1,0:T(8,128)(2,1)S(1)} %pad_maximum_fusion.1), channel_id=1, source_target_pairs={{0,1},{1,0},{2,3},{3,2},{4,5},{5,4},{6,7},{7,6},{8,9},{9,8},{10,11... | collective-permute-start | bytes 1572872 | tf_op jit(solution)/shard_map/ppermute | solution.py:204
  62.7 0.8 copy-start.4
  67.6 10.2 %all-to-all-start.1 = ((bf16[8,64,128]{2,1,0:T(8,128)(2,1)}), bf16[8,64,128]{2,1,0:T(8,128)(2,1)S(1)}, u32[]{:S(2)}, u32[]{:S(2)}) async-start(bf16[8,64,128]{2,1,0:T(8,128)(2,1)} %get-tuple-element.18), calls=%async_computation.1 | async-start | bytes 262144 | tf_op jit(solution)/shard_map/all_to_all | solution.py:25
  80.1 17.3 %all-to-all-start.2 = ((bf16[8,64,128]{2,1,0:T(8,128)(2,1)}), bf16[8,64,128]{2,1,0:T(8,128)(2,1)S(1)}, u32[]{:S(2)}, u32[]{:S(2)}) async-start(bf16[8,64,128]{2,1,0:T(8,128)(2,1)} %shard_map.168), calls=%async_computation.2 | async-start | bytes 262144 | tf_op jit(solution)/shard_map/all_to_all | solution.py:25
  83.5 13.8 %copy-start.1 = (bf16[64,8192]{1,0:T(8,128)(2,1)}, bf16[64,8192]{1,0:T(8,128)(2,1)S(1)}, u32[]{:S(2)}) copy-start(bf16[64,8192]{1,0:T(8,128)(2,1)S(1)} %pad_maximum_fusion.first_ref.refs_1_.refs_2_) | copy-start | bytes 3145732
  83.5 47.0 %collective-permute-start.11 = (bf16[64,8192]{1,0:T(8,128)(2,1)S(1)}, bf16[64,8192]{1,0:T(8,128)(2,1)S(1)}, u32[]{:S(2)}, u32[]{:S(2)}) collective-permute-start(bf16[64,8192]{1,0:T(8,128)(2,1)S(1)} %pad_maximum_fusion.first_ref.refs_1_.refs_2_), channel_id=1, source_target_pairs={{0,8},{8,0},{1,9},{9,1},{2,10},{10,2},{3,11},{11,3},{4,12},{12,4},... | collective-permute-start | bytes 3145736 | tf_op jit(solution)/shard_map/ppermute | solution.py:204
  100.9 17.7 %all-to-all-start.3 = ((bf16[16,64,128]{2,1,0:T(8,128)(2,1)}), bf16[16,64,128]{2,1,0:T(8,128)(2,1)S(1)}, u32[]{:S(2)}, u32[]{:S(2)}) async-start(bf16[16,64,128]{2,1,0:T(8,128)(2,1)} %get-tuple-element.20), calls=%async_computation.3 | async-start | bytes 524288 | tf_op jit(solution)/shard_map/all_to_all | solution.py:25
  121.0 17.7 %all-to-all-start.4 = ((bf16[16,64,128]{2,1,0:T(8,128)(2,1)}), bf16[16,64,128]{2,1,0:T(8,128)(2,1)S(1)}, u32[]{:S(2)}, u32[]{:S(2)}) async-start(bf16[16,64,128]{2,1,0:T(8,128)(2,1)} %shard_map.172), calls=%async_computation.4 | async-start | bytes 524288 | tf_op jit(solution)/shard_map/all_to_all | solution.py:25
  130.5 1.0 copy-start.3
  138.6 0.7 copy-start.7
  143.7 22.6 %all-to-all-start.5 = ((bf16[32,64,128]{2,1,0:T(8,128)(2,1)}), bf16[32,64,128]{2,1,0:T(8,128)(2,1)S(1)}, u32[]{:S(2)}, u32[]{:S(2)}) async-start(bf16[32,64,128]{2,1,0:T(8,128)(2,1)} %get-tuple-element.22), calls=%async_computation.5 | async-start | bytes 1048576 | tf_op jit(solution)/shard_map/all_to_all | solution.py:25
  166.3 0.8 copy-start.6
  226.5 21.1 %copy-start.14 = (bf16[64,128]{1,0:T(8,128)(2,1)S(1)}, bf16[64,128]{1,0:T(8,128)(2,1)}, u32[]{:S(2)}) copy-start(bf16[64,128]{1,0:T(8,128)(2,1)} %get-tuple-element.23) | copy-start | bytes 49156
  244.1 18.0 %all-to-all-start.11 = ((bf16[16,64,128]{2,1,0:T(8,128)(2,1)}), bf16[16,64,128]{2,1,0:T(8,128)(2,1)S(1)}, u32[]{:S(2)}, u32[]{:S(2)}) async-start(bf16[16,64,128]{2,1,0:T(8,128)(2,1)} %get-tuple-element.27), calls=%async_computation.11 | async-start | bytes 524288 | tf_op jit(solution)/shard_map/all_to_all | solution.py:25
  248.7 21.7 %collective-permute-start.12 = (bf16[64,128]{1,0:T(8,128)(2,1)S(1)}, bf16[64,128]{1,0:T(8,128)(2,1)S(1)}, u32[]{:S(2)}, u32[]{:S(2)}) collective-permute-start(bf16[64,128]{1,0:T(8,128)(2,1)S(1)} %broadcast_select_fusion.20), channel_id=1, source_target_pairs={{0,8},{8,0},{1,9},{9,1},{2,10},{10,2},{3,11},{11,3},{4,12},{12,4},... | collective-permute-start | bytes 49160 | tf_op jit(solution)/shard_map/ppermute | solution.py:204
  265.1 10.7 %all-to-all-start.12 = ((bf16[8,64,128]{2,1,0:T(8,128)(2,1)}), bf16[8,64,128]{2,1,0:T(8,128)(2,1)S(1)}, u32[]{:S(2)}, u32[]{:S(2)}) async-start(bf16[8,64,128]{2,1,0:T(8,128)(2,1)} %shard_map.183), calls=%async_computation.12 | async-start | bytes 262144 | tf_op jit(solution)/shard_map/all_to_all | solution.py:25
  278.0 11.8 %all-to-all-start.13 = ((bf16[8,64,128]{2,1,0:T(8,128)(2,1)}), bf16[8,64,128]{2,1,0:T(8,128)(2,1)S(1)}, u32[]{:S(2)}, u32[]{:S(2)}) async-start(bf16[8,64,128]{2,1,0:T(8,128)(2,1)} %get-tuple-element.30), calls=%async_computation.13 | async-start | bytes 262144 | tf_op jit(solution)/shard_map/all_to_all | solution.py:25
  282.3 6.7 %collective-permute-start.13 = (bf16[64,64]{1,0:T(8,128)(2,1)S(1)}, bf16[64,64]{1,0:T(8,128)(2,1)S(1)}, u32[]{:S(2)}, u32[]{:S(2)}) collective-permute-start(bf16[64,64]{1,0:T(8,128)(2,1)S(1)} %broadcast_select_fusion.4), channel_id=1, source_target_pairs={{0,8},{8,0},{1,9},{9,1},{2,10},{10,2},{3,11},{11,3},{4,12},{12,4},... | collective-permute-start | bytes 24584 | tf_op jit(solution)/shard_map/ppermute | solution.py:204
  292.9 9.7 %all-to-all-start.14 = ((bf16[8,32,128]{2,1,0:T(8,128)(2,1)}), bf16[8,32,128]{2,1,0:T(8,128)(2,1)S(1)}, u32[]{:S(2)}, u32[]{:S(2)}) async-start(bf16[8,32,128]{2,1,0:T(8,128)(2,1)} %shard_map.185), calls=%async_computation.14 | async-start | bytes 131072 | tf_op jit(solution)/shard_map/all_to_all | solution.py:25
  (7 other events, 4.6 us)
